TPU v7x, 32 devices: a whole 2x2x4 slice. The times are simulated.
32 devices in a mesh: slab: 8 (over y, x, core), wide: 4 (over z).
Axes of the slice: x: 2, y: 2, z: 4, core: 2. Of those that a mesh axis runs over, the one named last changes fastest.
Arguments:
- face_owner_state: bfloat16 [256, 16, 128], P(('slab', 'wide')), may hold values from -6 to 6
- face_neighbour_state: bfloat16 [256, 16, 128], P(('slab', 'wide')), may hold values from -6 to 6
- flux_linear: float32 [16, 16], replicated, may hold values from -1.5 to 1.5
- flux_quadratic: bfloat16 [16, 256], replicated, may hold values from -0.375 to 0.375
- species_weight: float32 [11], replicated, may hold values from 0.5 to 1.5
- cell_state: bfloat16 [512, 16, 128], P(('slab', 'wide')), may hold values from -6 to 6
- cell_tau: float32 [512, 128], P(('slab', 'wide')), may hold values from 0.5 to 4
- cell_rate: float32 [512, 128], P(('slab', 'wide')), may hold values from 0.5 to 2
- newton_residual: float32 [512, 16, 128], P(('slab', 'wide')), may hold values from -6 to 6
- tile_dest: int32 [256, 1], P(('slab', 'wide')), may hold values from 0 to 3; in each aligned block of 8 rows (0 to 7, 8 to 15, ...) at most 4 rows name the same one
- tile_row: int32 [256], P(('slab', 'wide')), may hold values from 0 to 15
- tile_nbr: int32 [256], P(('slab', 'wide')), may hold values from 0 to 23
- halo_list: int32 [32, 2, 4], P(('slab', 'wide')), may hold values from 0 to 15
Outputs:
- first_product: float32 [512, 16, 128], P(('slab', 'wide'))
- second_product: float32 [512, 16, 128], P(('slab', 'wide'))
Inputs may be any that keep to these rules, and one draw needn't show every extreme that they name: `tile_dest`: among the face tiles of one device no owner is named more than 4 times, and in some device some owner is named exactly 4 times.
All inputs are finite; a program needn't handle non-finite values.
Results may differ from a plain program's by a relative error of at most 0.008.
Values may be sent and summed in bfloat16 or wider, within the bound.
A program may use at most 64 MiB of HBM per device.

v0:
```python
import functools

import jax
import jax.numpy as jnp
from jax import lax
from jax.experimental import pallas as pl
from jax.experimental.pallas import tpu as pltpu
from jax.sharding import PartitionSpec as P

CAP = 4
MESH = pl.DeviceIdType.MESH
F32 = jnp.float32
BF16 = jnp.bfloat16


def each(low, high, body):
    if high - low <= 8:
        for i in range(low, high):
            body(i)
    else:

        def step(i, carry):
            body(i)
            return carry

        lax.fori_loop(low, high, step, 0)


def kernel(
    owners,
    slabs,
    fo_hbm,
    fn_hbm,
    lin_hbm,
    quad_hbm,
    weight_hbm,
    state_hbm,
    tau_hbm,
    rate_hbm,
    res_hbm,
    dest_hbm,
    row_hbm,
    nbr_hbm,
    halo_hbm,
    outv1,
    outv2,
    fo,
    fn,
    lin,
    quad,
    state,
    tau,
    rate,
    res,
    faces,
    got,
    uf,
    speed,
    meta,
    got_meta,
    flux,
    flin,
    coef,
    acc,
    part,
    vown1,
    vown2,
    ext1,
    ext2,
    stage1,
    stage2,
    in_sem,
    face_send,
    face_recv,
    meta_send,
    meta_recv,
    halo_send,
    halo_recv,
    token,
    weight_ref,
    dest_ref,
    row_ref,
    nbr_ref,
    halo_ref,
):
    s = lax.axis_index("slab")
    w = lax.axis_index("wide")
    count, width, tile = fo.shape
    rows = res.shape[0]
    nspec = weight_ref.shape[0]
    halo = halo_ref.shape[2]
    slots = owners * CAP

    barrier = pltpu.get_barrier_semaphore()
    ways = ((0, 1), (1, -1))

    def valid(at):
        return (at >= 0) & (at < owners)

    for off in range(1, owners):
        peer = lax.rem(w + off, owners)
        pl.semaphore_signal(barrier, inc=1, device_id=(s, peer), device_id_type=MESH)

    @pl.when(s > 0)
    def _():
        pl.semaphore_signal(barrier, inc=1, device_id=(s - 1, w), device_id_type=MESH)

    @pl.when(s < slabs - 1)
    def _():
        pl.semaphore_signal(barrier, inc=1, device_id=(s + 1, w), device_id_type=MESH)

    loads = []
    for i, (a, b) in enumerate(
        (
            (fo_hbm, fo),
            (fn_hbm, fn),
            (res_hbm, res),
            (quad_hbm, quad),
            (lin_hbm, lin),
            (state_hbm, state),
            (tau_hbm, tau),
            (rate_hbm, rate),
            (weight_hbm, weight_ref),
            (dest_hbm, dest_ref),
            (row_hbm, row_ref),
            (nbr_hbm, nbr_ref),
            (halo_hbm, halo_ref),
        )
    ):
        copy = pltpu.make_async_copy(a, b, in_sem.at[i])
        copy.start()
        loads.append(copy)

    bits = count.bit_length()
    mask = (1 << bits) - 1

    def picks(peer):
        packed = jnp.int32(0)
        for t in range(count):
            packed = jnp.where(dest_ref[t] == peer, packed * (1 << bits) + (t + 1), packed)
        return [(packed >> (bits * c)) & mask for c in range(CAP)]

    for load in loads[8:]:
        load.wait()
    loads[0].wait()
    loads[1].wait()

    def fill(off):
        d = lax.rem(w + off, owners)
        found = picks(d)
        for c in range(CAP):
            source = jnp.maximum(found[c] - 1, 0)
            row = jnp.where(found[c] > 0, row_ref[source], rows)
            nbr = jnp.where(found[c] > 0, nbr_ref[source], 0)
            if isinstance(off, int) and off == 0:
                got_meta[w, c] = row
                got_meta[w, CAP + c] = nbr
                got[w, c, 0] = fo[source]
                got[w, c, 1] = fn[source]
            else:
                meta[d, c] = row
                meta[d, CAP + c] = nbr
                faces[d, c, 0] = fo[source]
                faces[d, c, 1] = fn[source]

    fill(0)
    each(1, owners, fill)

    loads[2].wait()

    def round_rows(r, carry):
        vb = res[r].astype(BF16)
        vown1[r] = vb
        ext1[r] = vb
        return carry

    lax.fori_loop(0, rows, round_rows, 0, unroll=4)

    def up_copy(phase, stage, ext):
        return pltpu.make_async_remote_copy(
            src_ref=stage.at[0],
            dst_ref=ext.at[pl.ds(rows, halo)],
            send_sem=halo_send.at[phase, 0],
            recv_sem=halo_recv.at[phase, 0],
            device_id=(s + 1, w),
            device_id_type=MESH,
        )

    def down_copy(phase, stage, ext):
        return pltpu.make_async_remote_copy(
            src_ref=stage.at[1],
            dst_ref=ext.at[pl.ds(rows + halo, halo)],
            send_sem=halo_send.at[phase, 1],
            recv_sem=halo_recv.at[phase, 1],
            device_id=(s - 1, w),
            device_id_type=MESH,
        )

    def send_halo(phase, stage, ext):
        @pl.when(s < slabs - 1)
        def _():
            up_copy(phase, stage, ext).start()

        @pl.when(s > 0)
        def _():
            down_copy(phase, stage, ext).start()

        @pl.when(s == 0)
        def _():
            ext[pl.ds(rows, halo)] = jnp.zeros((halo, width, tile), BF16)

        @pl.when(s == slabs - 1)
        def _():
            ext[pl.ds(rows + halo, halo)] = jnp.zeros((halo, width, tile), BF16)

    def wait_halo(phase, stage, ext):
        @pl.when(s > 0)
        def _():
            up_copy(phase, stage, ext).wait_recv()
            down_copy(phase, stage, ext).wait_send()

        @pl.when(s < slabs - 1)
        def _():
            down_copy(phase, stage, ext).wait_recv()
            up_copy(phase, stage, ext).wait_send()

    def stage_halo(vown, stage):
        for h in range(halo):
            stage[0, h] = vown[halo_ref[0, 0, h]]
            stage[1, h] = vown[halo_ref[0, 1, h]]

    stage_halo(vown1, stage1)

    loads[3].wait()
    loads[4].wait()
    wide = width * width
    fq = quad[...].astype(F32) * 0.5
    own_lane = lax.broadcasted_iota(jnp.int32, (width, wide), 1) // width
    own_sub = lax.broadcasted_iota(jnp.int32, (width, wide), 0)
    keep = own_lane == own_sub
    lane_block = lax.broadcasted_iota(jnp.int32, (width, tile), 1) // width
    per = tile // width
    for half in range(wide // tile):
        total = jnp.zeros((width, tile), F32)
        for m in range(per):
            k = half * per + m
            spread = jnp.where(keep, jnp.broadcast_to(fq[k : k + 1, :], (width, wide)), 0.0)
            fold = spread[:, :tile]
            for piece in range(1, wide // tile):
                fold = fold + spread[:, piece * tile : (piece + 1) * tile]
            step = tile // 2
            while step >= width:
                fold = fold + pltpu.roll(fold, step, 1)
                step //= 2
            total = jnp.where(lane_block == m, fold, total)
        flux[:, half * tile : (half + 1) * tile] = total.astype(BF16)
    half_lin = lin[...] * 0.5
    high = half_lin.astype(BF16)
    flin[:, :width] = high
    flin[:, width:] = (half_lin - high.astype(F32)).astype(BF16)

    loads[5].wait()
    loads[6].wait()
    loads[7].wait()
    sub = lax.broadcasted_iota(jnp.int32, (width, tile), 0)
    relax = jnp.where(sub == 14, 1.0, 0.0) - jnp.where(sub == 15, 1.0, 0.0)
    mixture = jnp.zeros((width, tile), F32)
    for m in range(nspec):
        mixture = jnp.where(sub == m, weight_ref[m], mixture)

    def prepare(r, carry):
        u = state[r].astype(F32)
        inv = 1.0 / tau[pl.ds(r, 1), :]
        rho = jnp.sum(mixture * u, axis=0, keepdims=True) * inv
        gap = jnp.sum(relax * u, axis=0, keepdims=True) * inv
        coef[r] = gap * mixture + rho * relax
        return carry

    lax.fori_loop(0, rows, prepare, 0, unroll=4)

    def diagonal(vown):
        def one(r, carry):
            v = vown[r].astype(F32)
            change = jnp.sum(coef[r] * v, axis=0, keepdims=True)
            acc[r] = rate[pl.ds(r, 1), :] * v + relax * change
            return carry

        lax.fori_loop(0, rows, one, 0, unroll=4)

    diagonal(vown1)


    def face_copy(src, dst, peer):
        return pltpu.make_async_remote_copy(
            src_ref=faces.at[src],
            dst_ref=got.at[dst],
            send_sem=face_send.at[src],
            recv_sem=face_recv.at[dst],
            device_id=(s, peer),
            device_id_type=MESH,
        )

    def meta_copy(src, dst, peer):
        return pltpu.make_async_remote_copy(
            src_ref=meta.at[src],
            dst_ref=got_meta.at[dst],
            send_sem=meta_send.at[src],
            recv_sem=meta_recv.at[dst],
            device_id=(s, peer),
            device_id_type=MESH,
        )

    below = jnp.where(s > 0, 1, 0)
    above = jnp.where(s < slabs - 1, 1, 0)
    pl.semaphore_wait(barrier, owners - 1 + below + above)

    def send(delta):
        for way, sign in ways:
            peer = w + sign * delta

            @pl.when(valid(peer))
            def _():
                meta_copy(peer, w, peer).start()
                face_copy(peer, w, peer).start()

    each(1, owners, lambda i: send(owners - i))
    send_halo(0, stage1, ext1)

    def side(q, which, vectors):
        blocks = []
        for c in range(CAP):
            v = vectors[c]
            blocks.append(
                jnp.concatenate(
                    [
                        jnp.broadcast_to(uf[q, c, which, pl.ds(k, 1), :], (width, tile)).astype(BF16) * v
                        for k in range(width)
                    ],
                    axis=0,
                )
            )
        outer = jnp.concatenate(blocks, axis=1)
        plain = jnp.concatenate([jnp.concatenate([v, v], axis=0) for v in vectors], axis=1)
        return jnp.dot(flux[...], outer, preferred_element_type=F32) + jnp.dot(
            flin[...], plain, preferred_element_type=F32
        )

    def own_side(q, vown):
        vectors = [vown[jnp.minimum(got_meta[q, c], rows - 1)] for c in range(CAP)]
        out = side(q, 0, vectors)
        return [
            out[:, c * tile : (c + 1) * tile] + speed[q, pl.ds(c, 1), :] * vectors[c].astype(F32)
            for c in range(CAP)
        ]

    def nbr_side(q, ext):
        vectors = [ext[got_meta[q, CAP + c]] for c in range(CAP)]
        out = side(q, 1, vectors)
        return [
            out[:, c * tile : (c + 1) * tile] - speed[q, pl.ds(c, 1), :] * vectors[c].astype(F32)
            for c in range(CAP)
        ]

    def unpack(q):
        for c in range(CAP):
            own = got[q, c, 0].astype(F32)
            nbr = got[q, c, 1].astype(F32)
            uf[q, c, 0] = own
            uf[q, c, 1] = nbr
            square = jnp.sum(own * own + nbr * nbr, axis=0, keepdims=True)
            speed[q, pl.ds(c, 1), :] = 0.5 + 0.5 * jnp.sqrt(square * (0.5 / width))

    wait_halo(0, stage1, ext1)

    def first_part(off, carry):
        q = lax.rem(jnp.where(2 * w < owners, w + off, w + owners - off), owners)

        @pl.when(off > 0)
        def _():
            meta_copy(q, q, q).wait()
            face_copy(q, q, q).wait()

        unpack(q)
        a = own_side(q, vown1)
        b = nbr_side(q, ext1)
        for c in range(CAP):
            part[q, c] = a[c] + b[c]
        return carry

    lax.fori_loop(0, owners, first_part, 0)

    def collect():
        def one(q, totals):
            for c in range(CAP):
                term = part[q, c]
                at = got_meta[q, c]
                totals = tuple(t + jnp.where(at == r, term, 0.0) for r, t in enumerate(totals))
            return totals

        return lax.fori_loop(0, owners, one, tuple(acc[r] for r in range(rows)))

    for r, value in enumerate(collect()):
        outv1[r] = value
        vb = value.astype(BF16)
        vown2[r] = vb
        ext2[r] = vb
    stage_halo(vown2, stage2)
    send_halo(1, stage2, ext2)

    def second_own(q, carry):
        a = own_side(q, vown2)
        for c in range(CAP):
            part[q, c] = a[c]
        return carry

    lax.fori_loop(0, owners, second_own, 0, unroll=4)
    diagonal(vown2)
    wait_halo(1, stage2, ext2)

    def second_nbr(q, carry):
        b = nbr_side(q, ext2)
        for c in range(CAP):
            part[q, c] += b[c]
        return carry

    lax.fori_loop(0, owners, second_nbr, 0, unroll=4)
    for r, value in enumerate(collect()):
        outv2[r] = value

def store(a, b, c, d, sem):
    first = pltpu.make_async_copy(a, c, sem.at[0])
    second = pltpu.make_async_copy(b, d, sem.at[1])
    first.start()
    second.start()
    first.wait()
    second.wait()


def solution(mesh):
    owners = mesh.shape["wide"]
    slabs = mesh.shape["slab"]

    def on_device(fo, fn, lin, quad, weight, state, tau, rate, res, dest, row, nbr, halo_list):
        count, width, tile = fo.shape
        rows = res.shape[0]
        halo = halo_list.shape[2]
        hbm = pl.BlockSpec(memory_space=pltpu.MemorySpace.HBM)
        vmem = pl.BlockSpec(memory_space=pltpu.MemorySpace.VMEM)
        dma = pltpu.SemaphoreType.DMA
        row_set = (rows, width, tile)
        products = pl.pallas_call(
            functools.partial(kernel, owners, slabs),
            out_shape=(pltpu.VMEM(row_set, F32), pltpu.VMEM(row_set, F32)),
            in_specs=[hbm] * 13,
            out_specs=(vmem, vmem),
            scratch_shapes=[
                pltpu.VMEM(fo.shape, BF16),
                pltpu.VMEM(fn.shape, BF16),
                pltpu.VMEM(lin.shape, F32),
                pltpu.VMEM(quad.shape, BF16),
                pltpu.VMEM(state.shape, BF16),
                pltpu.VMEM(tau.shape, F32),
                pltpu.VMEM(rate.shape, F32),
                pltpu.VMEM(row_set, F32),
                pltpu.VMEM((owners, CAP, 2, width, tile), BF16),
                pltpu.VMEM((owners, CAP, 2, width, tile), BF16),
                pltpu.VMEM((owners, CAP, 2, width, tile), F32),
                pltpu.VMEM((owners, 8, tile), F32),
                pltpu.SMEM((owners, 2 * CAP), jnp.int32),
                pltpu.SMEM((owners, 2 * CAP), jnp.int32),
                pltpu.VMEM((width, width * width), BF16),
                pltpu.VMEM((width, 2 * width), BF16),
                pltpu.VMEM(row_set, F32),
                pltpu.VMEM(row_set, F32),
                pltpu.VMEM((owners, CAP, width, tile), F32),
                pltpu.VMEM(row_set, BF16),
                pltpu.VMEM(row_set, BF16),
                pltpu.VMEM((rows + 2 * halo, width, tile), BF16),
                pltpu.VMEM((rows + 2 * halo, width, tile), BF16),
                pltpu.VMEM((2, halo, width, tile), BF16),
                pltpu.VMEM((2, halo, width, tile), BF16),
                dma((13,)),
                dma((owners,)),
                dma((owners,)),
                dma((owners,)),
                dma((owners,)),
                dma((2, 2)),
                dma((2, 2)),
                pltpu.SemaphoreType.REGULAR((2, owners + 1)),
                pltpu.SMEM(weight.shape, F32),
                pltpu.SMEM((count,), jnp.int32),
                pltpu.SMEM(row.shape, jnp.int32),
                pltpu.SMEM(nbr.shape, jnp.int32),
                pltpu.SMEM(halo_list.shape, jnp.int32),
            ],
            compiler_params=pltpu.CompilerParams(collective_id=0, has_side_effects=True),
        )(fo, fn, lin, quad, weight, state, tau, rate, res, dest.reshape(count), row, nbr, halo_list)
        return pl.pallas_call(
            store,
            out_shape=(jax.ShapeDtypeStruct(row_set, F32), jax.ShapeDtypeStruct(row_set, F32)),
            in_specs=[vmem, vmem],
            out_specs=(hbm, hbm),
            scratch_shapes=[dma((2,))],
        )(*[pltpu.with_memory_space_constraint(x, pltpu.MemorySpace.VMEM) for x in products])

    every = ("slab", "wide")
    cube, flat = P(every, None, None), P(every, None)
    return jax.shard_map(
        on_device,
        mesh=mesh,
        in_specs=(cube, cube, P(), P(), P(), cube, flat, flat, cube, flat, P(every), P(every), cube),
        out_specs=(cube, cube),
        check_vma=False,
    )
```

profile of v0, /device:TPU:1, one launch (start us, length us, event | category | flops | bytes accessed | tf_op | source)
XLA Modules:
  0.0 14.2 jit_solution(4252262284778949380)
XLA Ops:
  0.6 12.9 %shard_map.140 = (f32[16,16,128]{2,1,0:T(8,128)S(1)}, f32[16,16,128]{2,1,0:T(8,128)S(1)}) custom-call(bf16[8,16,128]{2,1,0:T(8,128)(2,1)} %fo_hbm.1, bf16[8,16,128]{2,1,0:T(8,128)(2,1)} %fn_hbm.1, f32[16,16]{1,0:T(8,128)} %lin_hbm.1, bf16[16,256]{1,0:T(8,128)(2,1)} %quad_hbm.1, f32[11]{0:T(128)} %weight_hbm.1, bf16[16,16,128]{2,1,0:T(8,128)(2,1)} %state_hbm.1, ...), custom_call_target="tpu_custom_call" | custom-call | tf_op jit(solution)/shard_map/pallas_call | solution.py:451
  13.5 0.7 %shard_map.141 = (f32[16,16,128]{2,1,0:T(8,128)}, f32[16,16,128]{2,1,0:T(8,128)}) custom-call(f32[16,16,128]{2,1,0:T(8,128)S(1)} %get-tuple-element.4.a, f32[16,16,128]{2,1,0:T(8,128)S(1)} %get-tuple-element.5.b), custom_call_target="tpu_custom_call" | custom-call | tf_op jit(solution)/shard_map/pallas_call | solution.py:498
where the time goes:
time: 14.4 us; the launch traced here: 14.2 us
  Pallas kernels  13.6 us (94%)
  between operations  0.64 us (4%)
    pallas_call x1, Pallas kernels, on_device(): pl.pallas_call(functools.partial(kernel, owners, slabs), out_shape=(pltpu...  12.9 us
    pallas_call x1, Pallas kernels, on_device(): pl.pallas_call(store, out_shape=(jax.ShapeDtypeStruct(row_set, F32), jax....  0.72 us

commit v1 on v0

--- a/solution.py
+++ b/solution.py
@@ -62,7 +62,6 @@
     flin,
     coef,
     acc,
-    part,
     vown1,
     vown2,
     ext1,
@@ -76,7 +75,8 @@
     meta_recv,
     halo_send,
     halo_recv,
-    token,
+    ready,
+    halo_ready,
     weight_ref,
     dest_ref,
     row_ref,
@@ -89,31 +89,21 @@
     rows = res.shape[0]
     nspec = weight_ref.shape[0]
     halo = halo_ref.shape[2]
-    slots = owners * CAP
 
     barrier = pltpu.get_barrier_semaphore()
-    ways = ((0, 1), (1, -1))
-
-    def valid(at):
-        return (at >= 0) & (at < owners)
-
-    for off in range(1, owners):
-        peer = lax.rem(w + off, owners)
-        pl.semaphore_signal(barrier, inc=1, device_id=(s, peer), device_id_type=MESH)
-
-    @pl.when(s > 0)
-    def _():
-        pl.semaphore_signal(barrier, inc=1, device_id=(s - 1, w), device_id_type=MESH)
-
-    @pl.when(s < slabs - 1)
-    def _():
-        pl.semaphore_signal(barrier, inc=1, device_id=(s + 1, w), device_id_type=MESH)
+    even = lax.rem(s, 2) == 0
+    has_down = s > 0
+    has_up = s < slabs - 1
 
     loads = []
     for i, (a, b) in enumerate(
         (
+            (dest_hbm, dest_ref),
+            (row_hbm, row_ref),
+            (nbr_hbm, nbr_ref),
             (fo_hbm, fo),
             (fn_hbm, fn),
+            (halo_hbm, halo_ref),
             (res_hbm, res),
             (quad_hbm, quad),
             (lin_hbm, lin),
@@ -121,16 +111,55 @@
             (tau_hbm, tau),
             (rate_hbm, rate),
             (weight_hbm, weight_ref),
-            (dest_hbm, dest_ref),
-            (row_hbm, row_ref),
-            (nbr_hbm, nbr_ref),
-            (halo_hbm, halo_ref),
         )
     ):
         copy = pltpu.make_async_copy(a, b, in_sem.at[i])
         copy.start()
         loads.append(copy)
 
+    def signal(sem, slab, wide):
+        pl.semaphore_signal(sem, inc=1, device_id=(slab, wide), device_id_type=MESH)
+
+    def greet(off):
+        @pl.when(w + off < owners)
+        def _():
+            signal(barrier, s, w + off)
+
+    each(1, owners, greet)
+
+    @pl.when(jnp.logical_not(even))
+    def _():
+        signal(barrier, s - 1, w)
+
+        @pl.when(has_up)
+        def _():
+            signal(barrier, s + 1, w)
+
+    around = jnp.where(has_down, 1, 0) + jnp.where(has_up, 1, 0)
+    greeted = w + jnp.where(even, around, 0)
+
+    @pl.when(greeted > 0)
+    def _():
+        pl.semaphore_wait(barrier, greeted)
+
+
+    def answer(off):
+        @pl.when(w - off >= 0)
+        def _():
+            signal(ready.at[w], s, w - off)
+
+    each(1, owners, answer)
+
+    @pl.when(even)
+    def _():
+        @pl.when(has_down)
+        def _():
+            signal(halo_ready.at[1], s - 1, w)
+
+        @pl.when(has_up)
+        def _():
+            signal(halo_ready.at[0], s + 1, w)
+
     bits = count.bit_length()
     mask = (1 << bits) - 1
 
@@ -140,19 +169,13 @@
             packed = jnp.where(dest_ref[t] == peer, packed * (1 << bits) + (t + 1), packed)
         return [(packed >> (bits * c)) & mask for c in range(CAP)]
 
-    for load in loads[8:]:
-        load.wait()
-    loads[0].wait()
-    loads[1].wait()
-
-    def fill(off):
-        d = lax.rem(w + off, owners)
+    def fill(d, own):
         found = picks(d)
         for c in range(CAP):
             source = jnp.maximum(found[c] - 1, 0)
             row = jnp.where(found[c] > 0, row_ref[source], rows)
             nbr = jnp.where(found[c] > 0, nbr_ref[source], 0)
-            if isinstance(off, int) and off == 0:
+            if own:
                 got_meta[w, c] = row
                 got_meta[w, CAP + c] = nbr
                 got[w, c, 0] = fo[source]
@@ -163,18 +186,42 @@
                 faces[d, c, 0] = fo[source]
                 faces[d, c, 1] = fn[source]
 
-    fill(0)
-    each(1, owners, fill)
-
-    loads[2].wait()
-
-    def round_rows(r, carry):
-        vb = res[r].astype(BF16)
-        vown1[r] = vb
-        ext1[r] = vb
-        return carry
-
-    lax.fori_loop(0, rows, round_rows, 0, unroll=4)
+    def face_copy(src, dst, peer):
+        return pltpu.make_async_remote_copy(
+            src_ref=faces.at[src],
+            dst_ref=got.at[dst],
+            send_sem=face_send.at[src],
+            recv_sem=face_recv.at[dst],
+            device_id=(s, peer),
+            device_id_type=MESH,
+        )
+
+    def meta_copy(src, dst, peer):
+        return pltpu.make_async_remote_copy(
+            src_ref=meta.at[src],
+            dst_ref=got_meta.at[dst],
+            send_sem=meta_send.at[src],
+            recv_sem=meta_recv.at[dst],
+            device_id=(s, peer),
+            device_id_type=MESH,
+        )
+
+    def send(peer):
+        meta_copy(peer, w, peer).start()
+        face_copy(peer, w, peer).start()
+
+    for load in loads[:5]:
+        load.wait()
+
+    def send_lower(i):
+        peer = w - (owners - i)
+
+        @pl.when(peer >= 0)
+        def _():
+            fill(peer, False)
+            send(peer)
+
+    each(1, owners, send_lower)
 
     def up_copy(phase, stage, ext):
         return pltpu.make_async_remote_copy(
@@ -196,43 +243,77 @@
             device_id_type=MESH,
         )
 
-    def send_halo(phase, stage, ext):
-        @pl.when(s < slabs - 1)
+    def send_up(phase, stage, ext):
+        @pl.when(has_up)
         def _():
             up_copy(phase, stage, ext).start()
 
-        @pl.when(s > 0)
+    def send_down(phase, stage, ext):
+        @pl.when(has_down)
         def _():
             down_copy(phase, stage, ext).start()
 
-        @pl.when(s == 0)
-        def _():
-            ext[pl.ds(rows, halo)] = jnp.zeros((halo, width, tile), BF16)
-
-        @pl.when(s == slabs - 1)
-        def _():
-            ext[pl.ds(rows + halo, halo)] = jnp.zeros((halo, width, tile), BF16)
-
     def wait_halo(phase, stage, ext):
-        @pl.when(s > 0)
+        @pl.when(has_down)
         def _():
             up_copy(phase, stage, ext).wait_recv()
-            down_copy(phase, stage, ext).wait_send()
-
-        @pl.when(s < slabs - 1)
+
+        @pl.when(has_up)
         def _():
             down_copy(phase, stage, ext).wait_recv()
-            up_copy(phase, stage, ext).wait_send()
 
     def stage_halo(vown, stage):
         for h in range(halo):
             stage[0, h] = vown[halo_ref[0, 0, h]]
             stage[1, h] = vown[halo_ref[0, 1, h]]
 
+    loads[5].wait()
+    loads[6].wait()
+
+    def round_rows(r, carry):
+        vb = res[r].astype(BF16)
+        vown1[r] = vb
+        ext1[r] = vb
+        return carry
+
+    lax.fori_loop(0, rows, round_rows, 0, unroll=4)
     stage_halo(vown1, stage1)
 
-    loads[3].wait()
-    loads[4].wait()
+    @pl.when(even)
+    def _():
+        send_up(0, stage1, ext1)
+        send_down(0, stage1, ext1)
+
+    for ext in (ext1, ext2):
+
+        @pl.when(s == 0)
+        def _():
+            ext[pl.ds(rows, halo)] = jnp.zeros((halo, width, tile), BF16)
+
+        @pl.when(s == slabs - 1)
+        def _():
+            ext[pl.ds(rows + halo, halo)] = jnp.zeros((halo, width, tile), BF16)
+
+    def fill_higher(off):
+        @pl.when(w + off < owners)
+        def _():
+            fill(w + off, False)
+
+    each(1, owners, fill_higher)
+    fill(w, True)
+
+    def send_higher(off):
+        peer = w + off
+
+        @pl.when(peer < owners)
+        def _():
+            pl.semaphore_wait(ready.at[peer], 1)
+            send(peer)
+
+    send_higher(1)
+
+    loads[7].wait()
+    loads[8].wait()
     wide = width * width
     fq = quad[...].astype(F32) * 0.5
     own_lane = lax.broadcasted_iota(jnp.int32, (width, wide), 1) // width
@@ -259,9 +340,18 @@
     flin[:, :width] = high
     flin[:, width:] = (half_lin - high.astype(F32)).astype(BF16)
 
-    loads[5].wait()
-    loads[6].wait()
-    loads[7].wait()
+    @pl.when(jnp.logical_not(even))
+    def _():
+        pl.semaphore_wait(halo_ready.at[0], 1)
+        send_down(0, stage1, ext1)
+
+        @pl.when(has_up)
+        def _():
+            pl.semaphore_wait(halo_ready.at[1], 1)
+            send_up(0, stage1, ext1)
+
+    for load in loads[9:]:
+        load.wait()
     sub = lax.broadcasted_iota(jnp.int32, (width, tile), 0)
     relax = jnp.where(sub == 14, 1.0, 0.0) - jnp.where(sub == 15, 1.0, 0.0)
     mixture = jnp.zeros((width, tile), F32)
@@ -289,42 +379,7 @@
 
     diagonal(vown1)
 
-
-    def face_copy(src, dst, peer):
-        return pltpu.make_async_remote_copy(
-            src_ref=faces.at[src],
-            dst_ref=got.at[dst],
-            send_sem=face_send.at[src],
-            recv_sem=face_recv.at[dst],
-            device_id=(s, peer),
-            device_id_type=MESH,
-        )
-
-    def meta_copy(src, dst, peer):
-        return pltpu.make_async_remote_copy(
-            src_ref=meta.at[src],
-            dst_ref=got_meta.at[dst],
-            send_sem=meta_send.at[src],
-            recv_sem=meta_recv.at[dst],
-            device_id=(s, peer),
-            device_id_type=MESH,
-        )
-
-    below = jnp.where(s > 0, 1, 0)
-    above = jnp.where(s < slabs - 1, 1, 0)
-    pl.semaphore_wait(barrier, owners - 1 + below + above)
-
-    def send(delta):
-        for way, sign in ways:
-            peer = w + sign * delta
-
-            @pl.when(valid(peer))
-            def _():
-                meta_copy(peer, w, peer).start()
-                face_copy(peer, w, peer).start()
-
-    each(1, owners, lambda i: send(owners - i))
-    send_halo(0, stage1, ext1)
+    each(2, owners, send_higher)
 
     def side(q, which, vectors):
         blocks = []
@@ -361,6 +416,13 @@
             for c in range(CAP)
         ]
 
+    def add_rows(q, terms):
+        for r in range(rows):
+            total = acc[r]
+            for c in range(CAP):
+                total = total + jnp.where(got_meta[q, c] == r, terms[c], 0.0)
+            acc[r] = total
+
     def unpack(q):
         for c in range(CAP):
             own = got[q, c, 0].astype(F32)
@@ -371,61 +433,72 @@
             speed[q, pl.ds(c, 1), :] = 0.5 + 0.5 * jnp.sqrt(square * (0.5 / width))
 
     wait_halo(0, stage1, ext1)
+    near = jnp.minimum(w, owners - 1 - w)
 
     def first_part(off, carry):
-        q = lax.rem(jnp.where(2 * w < owners, w + off, w + owners - off), owners)
+        apart = jnp.where(off <= 2 * near, (off + 1) // 2, off - near)
+        below = jnp.where(off <= 2 * near, lax.rem(off, 2) == 1, 2 * w >= owners)
+        q = jnp.where(below, w - apart, w + apart)
 
         @pl.when(off > 0)
         def _():
-            meta_copy(q, q, q).wait()
-            face_copy(q, q, q).wait()
+            meta_copy(q, q, q).wait_recv()
+            face_copy(q, q, q).wait_recv()
 
         unpack(q)
         a = own_side(q, vown1)
         b = nbr_side(q, ext1)
-        for c in range(CAP):
-            part[q, c] = a[c] + b[c]
+        add_rows(q, [a[c] + b[c] for c in range(CAP)])
         return carry
 
     lax.fori_loop(0, owners, first_part, 0)
 
-    def collect():
-        def one(q, totals):
-            for c in range(CAP):
-                term = part[q, c]
-                at = got_meta[q, c]
-                totals = tuple(t + jnp.where(at == r, term, 0.0) for r, t in enumerate(totals))
-            return totals
-
-        return lax.fori_loop(0, owners, one, tuple(acc[r] for r in range(rows)))
-
-    for r, value in enumerate(collect()):
+    for r in range(rows):
+        value = acc[r]
         outv1[r] = value
         vb = value.astype(BF16)
         vown2[r] = vb
         ext2[r] = vb
     stage_halo(vown2, stage2)
-    send_halo(1, stage2, ext2)
+    send_up(1, stage2, ext2)
+    send_down(1, stage2, ext2)
+
+    diagonal(vown2)
 
     def second_own(q, carry):
-        a = own_side(q, vown2)
-        for c in range(CAP):
-            part[q, c] = a[c]
+        add_rows(q, own_side(q, vown2))
         return carry
 
     lax.fori_loop(0, owners, second_own, 0, unroll=4)
-    diagonal(vown2)
     wait_halo(1, stage2, ext2)
 
     def second_nbr(q, carry):
-        b = nbr_side(q, ext2)
-        for c in range(CAP):
-            part[q, c] += b[c]
+        add_rows(q, nbr_side(q, ext2))
         return carry
 
     lax.fori_loop(0, owners, second_nbr, 0, unroll=4)
-    for r, value in enumerate(collect()):
-        outv2[r] = value
+    for r in range(rows):
+        outv2[r] = acc[r]
+
+    def sent(off):
+        for peer in (w + off, w - off):
+
+            @pl.when((peer >= 0) & (peer < owners))
+            def _():
+                meta_copy(peer, w, peer).wait_send()
+                face_copy(peer, w, peer).wait_send()
+
+    each(1, owners, sent)
+    for phase, stage, ext in ((0, stage1, ext1), (1, stage2, ext2)):
+
+        @pl.when(has_up)
+        def _():
+            up_copy(phase, stage, ext).wait_send()
+
+        @pl.when(has_down)
+        def _():
+            down_copy(phase, stage, ext).wait_send()
+
 
 def store(a, b, c, d, sem):
     first = pltpu.make_async_copy(a, c, sem.at[0])
@@ -472,7 +545,6 @@
                 pltpu.VMEM((width, 2 * width), BF16),
                 pltpu.VMEM(row_set, F32),
                 pltpu.VMEM(row_set, F32),
-                pltpu.VMEM((owners, CAP, width, tile), F32),
                 pltpu.VMEM(row_set, BF16),
                 pltpu.VMEM(row_set, BF16),
                 pltpu.VMEM((rows + 2 * halo, width, tile), BF16),
@@ -486,7 +558,8 @@
                 dma((owners,)),
                 dma((2, 2)),
                 dma((2, 2)),
-                pltpu.SemaphoreType.REGULAR((2, owners + 1)),
+                pltpu.SemaphoreType.REGULAR((owners,)),
+                pltpu.SemaphoreType.REGULAR((2,)),
                 pltpu.SMEM(weight.shape, F32),
                 pltpu.SMEM((count,), jnp.int32),
                 pltpu.SMEM(row.shape, jnp.int32),

time: 14.4 us -> 13.4 us (0.931)
  Pallas kernels: 13.6 us -> 12.6 us
    pallas_call x1, Pallas kernels: 12.9 us -> 11.9 us  [on_device(): pl.pallas_call(functools.partial(kernel, owners, slabs), out_shape=(pltpu...]
where the time goes in v1:
time: 13.4 us; the launch traced here: 13.2 us
  Pallas kernels  12.6 us (94%)
  between operations  0.64 us (5%)
    pallas_call x1, Pallas kernels, on_device(): pl.pallas_call(functools.partial(kernel, owners, slabs), out_shape=(pltpu...  11.9 us
    pallas_call x1, Pallas kernels, on_device(): pl.pallas_call(store, out_shape=(jax.ShapeDtypeStruct(row_set, F32), jax....  0.72 us

profile of v1, /device:TPU:1, one launch (start us, length us, event | category | flops | bytes accessed | tf_op | source)
XLA Modules:
  0.0 13.2 jit_solution(9361780720441448053)
XLA Ops:
  0.6 11.9 %shard_map.140 = (f32[16,16,128]{2,1,0:T(8,128)S(1)}, f32[16,16,128]{2,1,0:T(8,128)S(1)}) custom-call(bf16[8,16,128]{2,1,0:T(8,128)(2,1)} %fo_hbm.1, bf16[8,16,128]{2,1,0:T(8,128)(2,1)} %fn_hbm.1, f32[16,16]{1,0:T(8,128)} %lin_hbm.1, bf16[16,256]{1,0:T(8,128)(2,1)} %quad_hbm.1, f32[11]{0:T(128)} %weight_hbm.1, bf16[16,16,128]{2,1,0:T(8,128)(2,1)} %state_hbm.1, ...), custom_call_target="tpu_custom_call" | custom-call | tf_op jit(solution)/shard_map/pallas_call | solution.py:524
  12.5 0.7 %shard_map.141 = (f32[16,16,128]{2,1,0:T(8,128)}, f32[16,16,128]{2,1,0:T(8,128)}) custom-call(f32[16,16,128]{2,1,0:T(8,128)S(1)} %get-tuple-element.4.a, f32[16,16,128]{2,1,0:T(8,128)S(1)} %get-tuple-element.5.b), custom_call_target="tpu_custom_call" | custom-call | tf_op jit(solution)/shard_map/pallas_call | solution.py:571

commit v2 on v1

v2 whole, which is shorter than its diff:
```python
import functools

import jax
import jax.numpy as jnp
from jax import lax
from jax.experimental import pallas as pl
from jax.experimental.pallas import tpu as pltpu
from jax.sharding import PartitionSpec as P

CAP = 4
MESH = pl.DeviceIdType.MESH
F32 = jnp.float32
BF16 = jnp.bfloat16


def each(low, high, body):
    if high - low <= 8:
        for i in range(low, high):
            body(i)
    else:

        def step(i, carry):
            body(i)
            return carry

        lax.fori_loop(low, high, step, 0)


def kernel(
    owners,
    slabs,
    fo_hbm,
    fn_hbm,
    lin_hbm,
    quad_hbm,
    weight_hbm,
    state_hbm,
    tau_hbm,
    rate_hbm,
    res_hbm,
    dest_hbm,
    row_hbm,
    nbr_hbm,
    halo_hbm,
    outv1,
    outv2,
    fo,
    fn,
    lin,
    quad,
    state,
    tau,
    rate,
    res,
    faces,
    got,
    speed,
    meta,
    got_meta,
    flux,
    mats,
    coef,
    acc,
    part,
    vf1,
    vf2,
    stage,
    land,
    face_send,
    face_recv,
    meta_send,
    meta_recv,
    halo_send,
    halo_recv,
    ready,
    halo_ready,
    weight_ref,
    dest_ref,
    row_ref,
    nbr_ref,
    halo_ref,
    latest,
    before,
    own_row,
    nbr_row,
):
    s = lax.axis_index("slab")
    w = lax.axis_index("wide")
    count, width, tile = fo.shape
    rows = res.shape[0]
    nspec = weight_ref.shape[0]
    halo = halo_ref.shape[2]
    wide = width * width
    first_slot = rows + 1

    barrier = pltpu.get_barrier_semaphore()
    even = lax.rem(s, 2) == 0
    has_down = s > 0
    has_up = s < slabs - 1
    inner = has_down & has_up

    def signal(sem, slab, wide):
        pl.semaphore_signal(sem, inc=1, device_id=(slab, wide), device_id_type=MESH)

    def greet(off):
        @pl.when(w + off < owners)
        def _():
            signal(barrier, s, w + off)

    def answer(off):
        @pl.when(w - off >= 0)
        def _():
            signal(ready.at[w - 1], s, w - off)

    bits = count.bit_length()
    mask = (1 << bits) - 1

    def picks(peer):
        packed = jnp.int32(0)
        for t in range(count):
            packed = jnp.where(dest_ref[t] == peer, packed * (1 << bits) + (t + 1), packed)
        return [(packed >> (bits * c)) & mask for c in range(CAP)]

    def fill(d, own):
        found = picks(d)
        for c in range(CAP):
            source = jnp.maximum(found[c] - 1, 0)
            row = jnp.where(found[c] > 0, row_ref[source], rows)
            nbr = jnp.where(found[c] > 0, nbr_ref[source], 0)
            if own:
                got_meta[w, c] = row
                got_meta[w, CAP + c] = nbr
                got[w, c, 0] = fo[source]
                got[w, c, 1] = fn[source]
            else:
                meta[d, c] = row
                meta[d, CAP + c] = nbr
                faces[d, c, 0] = fo[source]
                faces[d, c, 1] = fn[source]

    def order(peer):
        return peer - jnp.where(peer > w, 1, 0)

    def face_copy(peer):
        return pltpu.make_async_remote_copy(
            src_ref=faces.at[peer],
            dst_ref=got.at[w],
            send_sem=face_send,
            recv_sem=face_recv.at[w - jnp.where(w > peer, 1, 0)],
            device_id=(s, peer),
            device_id_type=MESH,
        )

    def meta_copy(peer):
        return pltpu.make_async_remote_copy(
            src_ref=meta.at[peer],
            dst_ref=got_meta.at[w],
            send_sem=meta_send,
            recv_sem=meta_recv.at[w - jnp.where(w > peer, 1, 0)],
            device_id=(s, peer),
            device_id_type=MESH,
        )

    def send(peer):
        meta_copy(peer).start()
        face_copy(peer).start()

    def send_lower(i):
        peer = w - (owners - i)

        @pl.when(peer >= 0)
        def _():
            fill(peer, False)
            send(peer)

    def fill_higher(off):
        @pl.when(w + off < owners)
        def _():
            fill(w + off, False)

    def send_higher(off):
        peer = w + off

        @pl.when(peer < owners)
        def _():
            pl.semaphore_wait(ready.at[peer - 1], 1)
            send(peer)

    def up_copy(phase):
        return pltpu.make_async_remote_copy(
            src_ref=stage.at[phase, 0],
            dst_ref=land.at[phase, 0],
            send_sem=halo_send,
            recv_sem=halo_recv.at[phase],
            device_id=(s + 1, w),
            device_id_type=MESH,
        )

    def down_copy(phase):
        return pltpu.make_async_remote_copy(
            src_ref=stage.at[phase, 1],
            dst_ref=land.at[phase, 1],
            send_sem=halo_send,
            recv_sem=halo_recv.at[phase],
            device_id=(s - 1, w),
            device_id_type=MESH,
        )

    def send_halo(phase):
        @pl.when(has_up)
        def _():
            up_copy(phase).start()

        @pl.when(has_down)
        def _():
            down_copy(phase).start()

    def settle(sem, many, few):
        @pl.when(inner)
        def _():
            pltpu.make_async_copy(many, many, sem).wait()

        @pl.when(jnp.logical_not(inner))
        def _():
            pltpu.make_async_copy(few, few, sem).wait()

    def take_halo(phase, vf):
        settle(halo_recv.at[phase], land.at[phase], land.at[phase, 0])

        @pl.when(has_down)
        def _():
            for h in range(halo):
                vf[rows + h] = land[phase, 0, h].astype(F32)

        @pl.when(has_up)
        def _():
            for h in range(halo):
                vf[rows + halo + h] = land[phase, 1, h].astype(F32)

    def link(off, q):
        named = [got_meta[q, c] for c in range(CAP)]
        at = first_slot + off * CAP
        for c in range(CAP):
            last = latest[named[c]]
            for e in range(c):
                last = jnp.where(named[e] == named[c], at + e, last)
            before[off * CAP + c] = last
            own_row[off * CAP + c] = jnp.minimum(named[c], rows - 1)
            nbr_row[off * CAP + c] = got_meta[q, CAP + c]
        for r in range(rows):
            last = latest[r]
            for c in range(CAP):
                last = jnp.where(named[c] == r, at + c, last)
            latest[r] = last

    def assemble(off, q):
        for c in range(CAP):
            own = got[q, c, 0].astype(F32)
            nbr = got[q, c, 1].astype(F32)
            square = jnp.sum(own * own + nbr * nbr, axis=0, keepdims=True)
            speed[off, pl.ds(c, 1), :] = 0.5 + 0.5 * jnp.sqrt(square * (0.5 / width))
        for c in range(CAP):
            states = jnp.concatenate([got[q, c, 0], got[q, c, 1]], axis=1)
            ones = jnp.ones((2 * width, 2 * tile), BF16)
            both = jnp.dot(flux[...], jnp.concatenate([states, ones], axis=0), preferred_element_type=F32)
            mats[off, c, 0] = both[:, :tile]
            mats[off, c, 1] = both[:, tile:]

    def times(off, c, side, vf, row, total):
        for j in range(width):
            block = mats[off, c, side, j * width : (j + 1) * width, :]
            total = total + block * jnp.broadcast_to(vf[row, pl.ds(j, 1), :], (width, tile))
        return total

    def owned(off, c, vf):
        row = own_row[off * CAP + c]
        return times(off, c, 0, vf, row, speed[off, pl.ds(c, 1), :] * vf[row])

    def neighboured(off, c, vf):
        row = nbr_row[off * CAP + c]
        return times(off, c, 1, vf, row, -speed[off, pl.ds(c, 1), :] * vf[row])

    def chain(off, c, term):
        acc[first_slot + off * CAP + c] = term + acc[before[off * CAP + c]]

    def run(in_sem):
        loads = [
            pltpu.make_async_copy(a, b, in_sem.at[i])
            for i, (a, b) in enumerate(
                (
                    (dest_hbm, dest_ref),
                    (row_hbm, row_ref),
                    (nbr_hbm, nbr_ref),
                    (fo_hbm, fo),
                    (fn_hbm, fn),
                    (halo_hbm, halo_ref),
                    (res_hbm, res),
                    (quad_hbm, quad),
                    (lin_hbm, lin),
                    (state_hbm, state),
                    (tau_hbm, tau),
                    (rate_hbm, rate),
                    (weight_hbm, weight_ref),
                )
            )
        ]
        for load in loads[:5]:
            load.start()
        each(1, owners, greet)

        @pl.when(jnp.logical_not(even))
        def _():
            signal(barrier, s - 1, w)

            @pl.when(has_up)
            def _():
                signal(barrier, s + 1, w)

        for load in loads[5:]:
            load.start()
        around = jnp.where(has_down, 1, 0) + jnp.where(has_up, 1, 0)
        greeted = w + jnp.where(even, around, 0)

        @pl.when(greeted > 0)
        def _():
            pl.semaphore_wait(barrier, greeted)

        each(1, owners, answer)

        @pl.when(even)
        def _():
            @pl.when(has_down)
            def _():
                signal(halo_ready.at[1], s - 1, w)

            @pl.when(has_up)
            def _():
                signal(halo_ready.at[0], s + 1, w)

        for load in loads[:5]:
            load.wait()
        each(1, owners, send_lower)
        loads[5].wait()
        loads[6].wait()

        def round_rows(r, carry):
            vf1[r] = res[r].astype(BF16).astype(F32)
            return carry

        lax.fori_loop(0, rows, round_rows, 0, unroll=4)
        for h in range(halo):
            stage[0, 0, h] = vf1[halo_ref[0, 0, h]].astype(BF16)
            stage[0, 1, h] = vf1[halo_ref[0, 1, h]].astype(BF16)

        @pl.when(even)
        def _():
            send_halo(0)

        each(1, owners, fill_higher)
        fill(w, True)
        send_higher(1)

        for r in range(rows + 1):
            latest[r] = r
        acc[rows] = jnp.zeros((width, tile), F32)
        for vf in (vf1, vf2):

            @pl.when(s == 0)
            def _():
                vf[pl.ds(rows, halo)] = jnp.zeros((halo, width, tile), F32)

            @pl.when(s == slabs - 1)
            def _():
                vf[pl.ds(rows + halo, halo)] = jnp.zeros((halo, width, tile), F32)

        loads[7].wait()
        loads[8].wait()
        at = lax.broadcasted_iota(jnp.int32, (wide, wide), 0)
        column = lax.broadcasted_iota(jnp.int32, (wide, wide), 1)
        swap = jnp.where(column == lax.rem(at, width) * width + at // width, 1.0, 0.0).astype(BF16)
        flux[:, :width] = (
            lax.dot_general(swap, quad[...], (((1,), (1,)), ((), ())), preferred_element_type=F32) * 0.5
        ).astype(BF16)
        half_lin = lin[...] * 0.5
        high = half_lin.astype(BF16)
        low = (half_lin - high.astype(F32)).astype(BF16)
        at = lax.broadcasted_iota(jnp.int32, (wide, width), 0)
        column = lax.broadcasted_iota(jnp.int32, (wide, width), 1)
        pick = jnp.where(column == lax.rem(at, width), 1.0, 0.0).astype(BF16)
        keep = column == at // width
        for i, term in enumerate((high, low)):
            flux[:, (1 + i) * width : (2 + i) * width] = jnp.where(
                keep, jnp.dot(pick, term, preferred_element_type=F32), 0.0
            ).astype(BF16)

        @pl.when(jnp.logical_not(even))
        def _():
            pl.semaphore_wait(halo_ready.at[0], 1)
            down_copy(0).start()

            @pl.when(has_up)
            def _():
                pl.semaphore_wait(halo_ready.at[1], 1)
                up_copy(0).start()

        for load in loads[9:]:
            load.wait()

    pl.run_scoped(run, pltpu.SemaphoreType.DMA((13,)))

    sub = lax.broadcasted_iota(jnp.int32, (width, tile), 0)
    relax = jnp.where(sub == 14, 1.0, 0.0) - jnp.where(sub == 15, 1.0, 0.0)
    mixture = jnp.zeros((width, tile), F32)
    for m in range(nspec):
        mixture = jnp.where(sub == m, weight_ref[m], mixture)

    def prepare(r, carry):
        u = state[r].astype(F32)
        inv = 1.0 / tau[pl.ds(r, 1), :]
        rho = jnp.sum(mixture * u, axis=0, keepdims=True) * inv
        gap = jnp.sum(relax * u, axis=0, keepdims=True) * inv
        coef[r] = gap * mixture + rho * relax
        return carry

    lax.fori_loop(0, rows, prepare, 0, unroll=4)

    def diagonal(vf):
        def one(r, carry):
            v = vf[r]
            change = jnp.sum(coef[r] * v, axis=0, keepdims=True)
            acc[r] = rate[pl.ds(r, 1), :] * v + relax * change
            return carry

        lax.fori_loop(0, rows, one, 0, unroll=4)

    diagonal(vf1)
    each(2, owners, send_higher)
    take_halo(0, vf1)
    near = jnp.minimum(w, owners - 1 - w)

    def first_part(off, carry):
        apart = jnp.where(off <= 2 * near, (off + 1) // 2, off - near)
        below = jnp.where(off <= 2 * near, lax.rem(off, 2) == 1, 2 * w >= owners)
        q = jnp.where(below, w - apart, w + apart)

        @pl.when(off > 0)
        def _():
            pltpu.make_async_copy(got_meta.at[q], got_meta.at[q], meta_recv.at[order(q)]).wait()

        link(off, q)

        @pl.when(off > 0)
        def _():
            pltpu.make_async_copy(got.at[q], got.at[q], face_recv.at[order(q)]).wait()

        assemble(off, q)
        for c in range(CAP):
            chain(off, c, owned(off, c, vf1) + neighboured(off, c, vf1))
        return carry

    lax.fori_loop(0, owners, first_part, 0)

    for h in range(halo):
        stage[1, 0, h] = acc[latest[halo_ref[0, 0, h]]].astype(BF16)
        stage[1, 1, h] = acc[latest[halo_ref[0, 1, h]]].astype(BF16)
    send_halo(1)
    for r in range(rows):
        value = acc[latest[r]]
        outv1[r] = value
        vf2[r] = value.astype(BF16).astype(F32)
    diagonal(vf2)

    def second_own(off, carry):
        for c in range(CAP):
            part[off * CAP + c] = owned(off, c, vf2)
        return carry

    lax.fori_loop(0, owners, second_own, 0)
    pltpu.make_async_copy(faces.at[pl.ds(0, owners - 1)], faces.at[pl.ds(0, owners - 1)], face_send).wait()
    pltpu.make_async_copy(meta.at[pl.ds(0, owners - 1)], meta.at[pl.ds(0, owners - 1)], meta_send).wait()
    take_halo(1, vf2)

    def second_nbr(off, carry):
        for c in range(CAP):
            chain(off, c, part[off * CAP + c] + neighboured(off, c, vf2))
        return carry

    lax.fori_loop(0, owners, second_nbr, 0, unroll=4)
    for r in range(rows):
        outv2[r] = acc[latest[r]]
    settle(halo_send, stage, stage.at[0])


def store(a, b, c, d, sem):
    first = pltpu.make_async_copy(a, c, sem.at[0])
    second = pltpu.make_async_copy(b, d, sem.at[1])
    first.start()
    second.start()
    first.wait()
    second.wait()


def solution(mesh):
    owners = mesh.shape["wide"]
    slabs = mesh.shape["slab"]

    def on_device(fo, fn, lin, quad, weight, state, tau, rate, res, dest, row, nbr, halo_list):
        count, width, tile = fo.shape
        rows = res.shape[0]
        halo = halo_list.shape[2]
        hbm = pl.BlockSpec(memory_space=pltpu.MemorySpace.HBM)
        vmem = pl.BlockSpec(memory_space=pltpu.MemorySpace.VMEM)
        dma = pltpu.SemaphoreType.DMA
        row_set = (rows, width, tile)
        products = pl.pallas_call(
            functools.partial(kernel, owners, slabs),
            out_shape=(pltpu.VMEM(row_set, F32), pltpu.VMEM(row_set, F32)),
            in_specs=[hbm] * 13,
            out_specs=(vmem, vmem),
            scratch_shapes=[
                pltpu.VMEM(fo.shape, BF16),
                pltpu.VMEM(fn.shape, BF16),
                pltpu.VMEM(lin.shape, F32),
                pltpu.VMEM(quad.shape, BF16),
                pltpu.VMEM(state.shape, BF16),
                pltpu.VMEM(tau.shape, F32),
                pltpu.VMEM(rate.shape, F32),
                pltpu.VMEM(row_set, F32),
                pltpu.VMEM((owners, CAP, 2, width, tile), BF16),
                pltpu.VMEM((owners, CAP, 2, width, tile), BF16),
                pltpu.VMEM((owners, 8, tile), F32),
                pltpu.SMEM((owners, 2 * CAP), jnp.int32),
                pltpu.SMEM((owners, 2 * CAP), jnp.int32),
                pltpu.VMEM((width * width, 3 * width), BF16),
                pltpu.VMEM((owners, CAP, 2, width * width, tile), F32),
                pltpu.VMEM(row_set, F32),
                pltpu.VMEM((rows + 1 + owners * CAP, width, tile), F32),
                pltpu.VMEM((owners * CAP, width, tile), F32),
                pltpu.VMEM((rows + 2 * halo, width, tile), F32),
                pltpu.VMEM((rows + 2 * halo, width, tile), F32),
                pltpu.VMEM((2, 2, halo, width, tile), BF16),
                pltpu.VMEM((2, 2, halo, width, tile), BF16),
                dma(()),
                dma((owners - 1,)),
                dma(()),
                dma((owners - 1,)),
                dma(()),
                dma((2,)),
                pltpu.SemaphoreType.REGULAR((owners - 1,)),
                pltpu.SemaphoreType.REGULAR((2,)),
                pltpu.SMEM(weight.shape, F32),
                pltpu.SMEM((count,), jnp.int32),
                pltpu.SMEM(row.shape, jnp.int32),
                pltpu.SMEM(nbr.shape, jnp.int32),
                pltpu.SMEM(halo_list.shape, jnp.int32),
                pltpu.SMEM((rows + 1,), jnp.int32),
                pltpu.SMEM((owners * CAP,), jnp.int32),
                pltpu.SMEM((owners * CAP,), jnp.int32),
                pltpu.SMEM((owners * CAP,), jnp.int32),
            ],
            compiler_params=pltpu.CompilerParams(collective_id=0, has_side_effects=True),
        )(fo, fn, lin, quad, weight, state, tau, rate, res, dest.reshape(count), row, nbr, halo_list)
        return pl.pallas_call(
            store,
            out_shape=(jax.ShapeDtypeStruct(row_set, F32), jax.ShapeDtypeStruct(row_set, F32)),
            in_specs=[vmem, vmem],
            out_specs=(hbm, hbm),
            scratch_shapes=[dma((2,))],
        )(*[pltpu.with_memory_space_constraint(x, pltpu.MemorySpace.VMEM) for x in products])

    every = ("slab", "wide")
    cube, flat = P(every, None, None), P(every, None)
    return jax.shard_map(
        on_device,
        mesh=mesh,
        in_specs=(cube, cube, P(), P(), P(), cube, flat, flat, cube, flat, P(every), P(every), cube),
        out_specs=(cube, cube),
        check_vma=False,
    )
```

time: 13.4 us -> 12.7 us (0.948)
  Pallas kernels: 12.6 us -> 11.9 us
    pallas_call x1, Pallas kernels: 11.9 us -> 11.2 us  [on_device(): pl.pallas_call(functools.partial(kernel, owners, slabs), out_shape=(pltpu...]
where the time goes in v2:
time: 12.7 us; the launch traced here: 12.6 us
  Pallas kernels  11.9 us (94%)
  between operations  0.64 us (5%)
    pallas_call x1, Pallas kernels, on_device(): pl.pallas_call(functools.partial(kernel, owners, slabs), out_shape=(pltpu...  11.2 us
    pallas_call x1, Pallas kernels, on_device(): pl.pallas_call(store, out_shape=(jax.ShapeDtypeStruct(row_set, F32), jax....  0.72 us

profile of v2, /device:TPU:1, one launch (start us, length us, event | category | flops | bytes accessed | tf_op | source)
XLA Modules:
  0.0 12.6 jit_solution(883049300288474850)
XLA Ops:
  0.6 11.2 %shard_map.140 = (f32[16,16,128]{2,1,0:T(8,128)S(1)}, f32[16,16,128]{2,1,0:T(8,128)S(1)}) custom-call(bf16[8,16,128]{2,1,0:T(8,128)(2,1)} %fo_hbm.1, bf16[8,16,128]{2,1,0:T(8,128)(2,1)} %fn_hbm.1, f32[16,16]{1,0:T(8,128)} %lin_hbm.1, bf16[16,256]{1,0:T(8,128)(2,1)} %quad_hbm.1, f32[11]{0:T(128)} %weight_hbm.1, bf16[16,16,128]{2,1,0:T(8,128)(2,1)} %state_hbm.1, ...), custom_call_target="tpu_custom_call" | custom-call | tf_op jit(solution)/shard_map/pallas_call | solution.py:515
  11.8 0.7 %shard_map.141 = (f32[16,16,128]{2,1,0:T(8,128)}, f32[16,16,128]{2,1,0:T(8,128)}) custom-call(f32[16,16,128]{2,1,0:T(8,128)S(1)} %get-tuple-element.4.a, f32[16,16,128]{2,1,0:T(8,128)S(1)} %get-tuple-element.5.b), custom_call_target="tpu_custom_call" | custom-call | tf_op jit(solution)/shard_map/pallas_call | solution.py:563

commit v3 on v2

--- a/solution.py
+++ b/solution.py
@@ -57,7 +57,12 @@
     speed,
     meta,
     got_meta,
+    uf,
     flux,
+    form,
+    bilinear,
+    linear,
+    flin,
     mats,
     coef,
     acc,
@@ -207,13 +212,13 @@
         )
 
     def send_halo(phase):
+        @pl.when(has_down)
+        def _():
+            down_copy(phase).start()
+
         @pl.when(has_up)
         def _():
             up_copy(phase).start()
-
-        @pl.when(has_down)
-        def _():
-            down_copy(phase).start()
 
     def settle(sem, many, few):
         @pl.when(inner)
@@ -253,32 +258,65 @@
                 last = jnp.where(named[c] == r, at + c, last)
             latest[r] = last
 
-    def assemble(off, q):
+    def unpack(off, q):
         for c in range(CAP):
             own = got[q, c, 0].astype(F32)
             nbr = got[q, c, 1].astype(F32)
+            uf[off, c, 0] = own
+            uf[off, c, 1] = nbr
             square = jnp.sum(own * own + nbr * nbr, axis=0, keepdims=True)
             speed[off, pl.ds(c, 1), :] = 0.5 + 0.5 * jnp.sqrt(square * (0.5 / width))
+
+    def contract(low, high, vf):
+        def pair(i, carry):
+            at = low + 2 * i
+            vectors = jnp.concatenate([vf[at].astype(BF16), vf[at + 1].astype(BF16)], axis=1)
+            filled = jnp.dot(form[...], vectors, preferred_element_type=F32)
+            bilinear[at] = filled[:, :tile]
+            bilinear[at + 1] = filled[:, tile:]
+            flat = jnp.dot(flin[...], jnp.concatenate([vectors, vectors], axis=0), preferred_element_type=F32)
+            linear[at] = flat[:, :tile]
+            linear[at + 1] = flat[:, tile:]
+            return carry
+
+        lax.fori_loop(0, (high - low) // 2, pair, 0, unroll=2)
+
+    def applied(off, c, side, row):
+        total = linear[row]
+        for k in range(width):
+            block = bilinear[row, k * width : (k + 1) * width, :]
+            total = total + block * jnp.broadcast_to(uf[off, c, side, pl.ds(k, 1), :], (width, tile))
+        return total
+
+    def assemble(off, q):
+        states = jnp.concatenate([got[q, c, 1] for c in range(CAP)], axis=1)
+        ones = jnp.ones((2 * width, CAP * tile), BF16)
+        grown = jnp.dot(flux[...], jnp.concatenate([states, ones], axis=0), preferred_element_type=F32)
         for c in range(CAP):
-            states = jnp.concatenate([got[q, c, 0], got[q, c, 1]], axis=1)
-            ones = jnp.ones((2 * width, 2 * tile), BF16)
-            both = jnp.dot(flux[...], jnp.concatenate([states, ones], axis=0), preferred_element_type=F32)
-            mats[off, c, 0] = both[:, :tile]
-            mats[off, c, 1] = both[:, tile:]
-
-    def times(off, c, side, vf, row, total):
+            mats[off, c] = grown[:, c * tile : (c + 1) * tile]
+
+    def neighboured(off, c, vf):
+        row = nbr_row[off * CAP + c]
+        total = -speed[off, pl.ds(c, 1), :] * vf[row]
         for j in range(width):
-            block = mats[off, c, side, j * width : (j + 1) * width, :]
+            block = mats[off, c, j * width : (j + 1) * width, :]
             total = total + block * jnp.broadcast_to(vf[row, pl.ds(j, 1), :], (width, tile))
         return total
 
-    def owned(off, c, vf):
-        row = own_row[off * CAP + c]
-        return times(off, c, 0, vf, row, speed[off, pl.ds(c, 1), :] * vf[row])
-
-    def neighboured(off, c, vf):
-        row = nbr_row[off * CAP + c]
-        return times(off, c, 1, vf, row, -speed[off, pl.ds(c, 1), :] * vf[row])
+    def first_block(off, q):
+        link(off, q)
+        unpack(off, q)
+        for c in range(CAP):
+            row = jnp.minimum(got_meta[q, c], rows - 1)
+            nbr = got_meta[q, CAP + c]
+            jump = speed[off, pl.ds(c, 1), :] * (vf1[row] - vf1[nbr])
+            chain(off, c, (applied(off, c, 0, row) + jump) + applied(off, c, 1, nbr))
+
+    def source(off):
+        near = jnp.minimum(w, owners - 1 - w)
+        apart = jnp.where(off <= 2 * near, (off + 1) // 2, off - near)
+        below = jnp.where(off <= 2 * near, lax.rem(off, 2) == 1, 2 * w >= owners)
+        return jnp.where(below, w - apart, w + apart)
 
     def chain(off, c, term):
         acc[first_slot + off * CAP + c] = term + acc[before[off * CAP + c]]
@@ -388,10 +426,21 @@
         column = lax.broadcasted_iota(jnp.int32, (wide, width), 1)
         pick = jnp.where(column == lax.rem(at, width), 1.0, 0.0).astype(BF16)
         keep = column == at // width
+        flin[:, :width] = high
+        flin[:, width:] = low
         for i, term in enumerate((high, low)):
             flux[:, (1 + i) * width : (2 + i) * width] = jnp.where(
                 keep, jnp.dot(pick, term, preferred_element_type=F32), 0.0
             ).astype(BF16)
+        repeat = jnp.where(column == at // width, 1.0, 0.0).astype(BF16)
+        each_state = jnp.dot(repeat, quad[...], preferred_element_type=F32) * 0.5
+        at = lax.broadcasted_iota(jnp.int32, (wide, wide), 0)
+        column = lax.broadcasted_iota(jnp.int32, (wide, wide), 1)
+        each_state = jnp.where(column // width == lax.rem(at, width), each_state, 0.0).astype(BF16)
+        at = lax.broadcasted_iota(jnp.int32, (wide, width), 0)
+        column = lax.broadcasted_iota(jnp.int32, (wide, width), 1)
+        gather = jnp.where(column == lax.rem(at, width), 1.0, 0.0).astype(BF16)
+        form[...] = jnp.dot(each_state, gather, preferred_element_type=F32).astype(BF16)
 
         @pl.when(jnp.logical_not(even))
         def _():
@@ -434,45 +483,38 @@
         lax.fori_loop(0, rows, one, 0, unroll=4)
 
     diagonal(vf1)
+    contract(0, rows, vf1)
     each(2, owners, send_higher)
+
     take_halo(0, vf1)
-    near = jnp.minimum(w, owners - 1 - w)
+    contract(rows, rows + 2 * halo, vf1)
+    first_block(0, w)
 
     def first_part(off, carry):
-        apart = jnp.where(off <= 2 * near, (off + 1) // 2, off - near)
-        below = jnp.where(off <= 2 * near, lax.rem(off, 2) == 1, 2 * w >= owners)
-        q = jnp.where(below, w - apart, w + apart)
-
-        @pl.when(off > 0)
-        def _():
-            pltpu.make_async_copy(got_meta.at[q], got_meta.at[q], meta_recv.at[order(q)]).wait()
-
-        link(off, q)
-
-        @pl.when(off > 0)
-        def _():
-            pltpu.make_async_copy(got.at[q], got.at[q], face_recv.at[order(q)]).wait()
-
-        assemble(off, q)
-        for c in range(CAP):
-            chain(off, c, owned(off, c, vf1) + neighboured(off, c, vf1))
+        q = source(off)
+        pltpu.make_async_copy(got_meta.at[q], got_meta.at[q], meta_recv.at[order(q)]).wait()
+        pltpu.make_async_copy(got.at[q], got.at[q], face_recv.at[order(q)]).wait()
+        first_block(off, q)
         return carry
 
-    lax.fori_loop(0, owners, first_part, 0)
+    lax.fori_loop(1, owners, first_part, 0)
 
     for h in range(halo):
+        stage[1, 1, h] = acc[latest[halo_ref[0, 1, h]]].astype(BF16)
         stage[1, 0, h] = acc[latest[halo_ref[0, 0, h]]].astype(BF16)
-        stage[1, 1, h] = acc[latest[halo_ref[0, 1, h]]].astype(BF16)
     send_halo(1)
     for r in range(rows):
         value = acc[latest[r]]
         outv1[r] = value
         vf2[r] = value.astype(BF16).astype(F32)
     diagonal(vf2)
+    contract(0, rows, vf2)
 
     def second_own(off, carry):
         for c in range(CAP):
-            part[off * CAP + c] = owned(off, c, vf2)
+            row = own_row[off * CAP + c]
+            part[off * CAP + c] = applied(off, c, 0, row) + speed[off, pl.ds(c, 1), :] * vf2[row]
+        assemble(off, source(off))
         return carry
 
     lax.fori_loop(0, owners, second_own, 0)
@@ -531,8 +573,13 @@
                 pltpu.VMEM((owners, 8, tile), F32),
                 pltpu.SMEM((owners, 2 * CAP), jnp.int32),
                 pltpu.SMEM((owners, 2 * CAP), jnp.int32),
+                pltpu.VMEM((owners, CAP, 2, width, tile), F32),
                 pltpu.VMEM((width * width, 3 * width), BF16),
-                pltpu.VMEM((owners, CAP, 2, width * width, tile), F32),
+                pltpu.VMEM((width * width, width), BF16),
+                pltpu.VMEM((rows + 2 * halo, width * width, tile), F32),
+                pltpu.VMEM((rows + 2 * halo, width, tile), F32),
+                pltpu.VMEM((width, 2 * width), BF16),
+                pltpu.VMEM((owners, CAP, width * width, tile), F32),
                 pltpu.VMEM(row_set, F32),
                 pltpu.VMEM((rows + 1 + owners * CAP, width, tile), F32),
                 pltpu.VMEM((owners * CAP, width, tile), F32),

time: 12.7 us -> 12.6 us (level)
    pallas_call x1, Pallas kernels: 11.2 us -> 11 us  [on_device(): pl.pallas_call(functools.partial(kernel, owners, slabs), out_shape=(pltpu...]
where the time goes in v3:
time: 12.6 us; the launch traced here: 12.4 us
  Pallas kernels  11.8 us (94%)
  between operations  0.64 us (5%)
    pallas_call x1, Pallas kernels, on_device(): pl.pallas_call(functools.partial(kernel, owners, slabs), out_shape=(pltpu...  11 us
    pallas_call x1, Pallas kernels, on_device(): pl.pallas_call(store, out_shape=(jax.ShapeDtypeStruct(row_set, F32), jax....  0.72 us

profile of v3, /device:TPU:1, one launch (start us, length us, event | category | flops | bytes accessed | tf_op | source)
XLA Modules:
  0.0 12.4 jit_solution(15841069332168305167)
XLA Ops:
  0.6 11.0 %shard_map.140 = (f32[16,16,128]{2,1,0:T(8,128)S(1)}, f32[16,16,128]{2,1,0:T(8,128)S(1)}) custom-call(bf16[8,16,128]{2,1,0:T(8,128)(2,1)} %fo_hbm.1, bf16[8,16,128]{2,1,0:T(8,128)(2,1)} %fn_hbm.1, f32[16,16]{1,0:T(8,128)} %lin_hbm.1, bf16[16,256]{1,0:T(8,128)(2,1)} %quad_hbm.1, f32[11]{0:T(128)} %weight_hbm.1, bf16[16,16,128]{2,1,0:T(8,128)(2,1)} %state_hbm.1, ...), custom_call_target="tpu_custom_call" | custom-call | tf_op jit(solution)/shard_map/pallas_call | solution.py:557
  11.7 0.7 %shard_map.141 = (f32[16,16,128]{2,1,0:T(8,128)}, f32[16,16,128]{2,1,0:T(8,128)}) custom-call(f32[16,16,128]{2,1,0:T(8,128)S(1)} %get-tuple-element.4.a, f32[16,16,128]{2,1,0:T(8,128)S(1)} %get-tuple-element.5.b), custom_call_target="tpu_custom_call" | custom-call | tf_op jit(solution)/shard_map/pallas_call | solution.py:610

commit v4 on v2

v4 whole, which is shorter than its diff:
```python
import functools

import jax
import jax.numpy as jnp
from jax import lax
from jax.experimental import pallas as pl
from jax.experimental.pallas import tpu as pltpu
from jax.sharding import PartitionSpec as P

CAP = 4
MESH = pl.DeviceIdType.MESH
F32 = jnp.float32
BF16 = jnp.bfloat16


def each(low, high, body):
    if high - low <= 8:
        for i in range(low, high):
            body(i)
    else:

        def step(i, carry):
            body(i)
            return carry

        lax.fori_loop(low, high, step, 0)


def kernel(
    owners,
    slabs,
    fo_hbm,
    fn_hbm,
    lin_hbm,
    quad_hbm,
    weight_hbm,
    state_hbm,
    tau_hbm,
    rate_hbm,
    res_hbm,
    dest_hbm,
    row_hbm,
    nbr_hbm,
    halo_hbm,
    outv1,
    outv2,
    fo,
    fn,
    lin,
    quad,
    state,
    tau,
    rate,
    res,
    faces,
    got,
    speed,
    meta,
    got_meta,
    uf,
    flux,
    form,
    bilinear,
    linear,
    flin,
    mats,
    coef,
    acc,
    part,
    vf1,
    vf2,
    stage,
    land,
    face_recv,
    meta_recv,
    halo_recv,
    ready,
    halo_ready,
    weight_ref,
    dest_ref,
    row_ref,
    nbr_ref,
    halo_ref,
    latest,
    before,
    own_row,
    nbr_row,
    picked,
):
    def scope(in_sem, face_send, meta_send, halo_send):
        s = lax.axis_index("slab")
        w = lax.axis_index("wide")
        count, width, tile = fo.shape
        rows = res.shape[0]
        nspec = weight_ref.shape[0]
        halo = halo_ref.shape[2]
        wide = width * width
        first_slot = rows + 1

        barrier = pltpu.get_barrier_semaphore()
        even = lax.rem(s, 2) == 0
        has_down = s > 0
        has_up = s < slabs - 1
        inner = has_down & has_up

        def signal(sem, slab, wide):
            pl.semaphore_signal(sem, inc=1, device_id=(slab, wide), device_id_type=MESH)

        def greet(off):
            @pl.when(w + off < owners)
            def _():
                signal(barrier, s, w + off)

        def answer(off):
            @pl.when(w - off >= 0)
            def _():
                signal(ready.at[w - 1], s, w - off)

        bits = count.bit_length()
        mask = (1 << bits) - 1

        def picks(peer):
            packed = jnp.int32(0)
            for t in range(count):
                packed = jnp.where(dest_ref[t] == peer, packed * (1 << bits) + (t + 1), packed)
            return [(packed >> (bits * c)) & mask for c in range(CAP)]

        def fill_meta(d, place):
            found = picks(d)
            for c in range(CAP):
                source = jnp.maximum(found[c] - 1, 0)
                picked[d, c] = source
                place[d, c] = jnp.where(found[c] > 0, row_ref[source], rows)
                place[d, CAP + c] = jnp.where(found[c] > 0, nbr_ref[source], 0)

        def fill_faces(d, place):
            for c in range(CAP):
                source = picked[d, c]
                place[d, c, 0] = fo[source]
                place[d, c, 1] = fn[source]

        def order(peer):
            return peer - jnp.where(peer > w, 1, 0)

        def face_copy(peer):
            return pltpu.make_async_remote_copy(
                src_ref=faces.at[peer],
                dst_ref=got.at[w],
                send_sem=face_send,
                recv_sem=face_recv.at[w - jnp.where(w > peer, 1, 0)],
                device_id=(s, peer),
                device_id_type=MESH,
            )

        def meta_copy(peer):
            return pltpu.make_async_remote_copy(
                src_ref=meta.at[peer],
                dst_ref=got_meta.at[w],
                send_sem=meta_send,
                recv_sem=meta_recv.at[w - jnp.where(w > peer, 1, 0)],
                device_id=(s, peer),
                device_id_type=MESH,
            )

        def name_lower(peer):
            @pl.when(peer < w)
            def _():
                fill_meta(peer, meta)
                meta_copy(peer).start()

        def send_lower(peer):
            @pl.when(peer < w)
            def _():
                fill_faces(peer, faces)
                face_copy(peer).start()

        def fill_higher(off):
            @pl.when(w + off < owners)
            def _():
                fill_meta(w + off, meta)
                fill_faces(w + off, faces)

        def send_higher(off):
            peer = w + off

            @pl.when(peer < owners)
            def _():
                pl.semaphore_wait(ready.at[peer - 1], 1)
                meta_copy(peer).start()
                face_copy(peer).start()

        def up_copy(phase):
            return pltpu.make_async_remote_copy(
                src_ref=stage.at[phase, 0],
                dst_ref=land.at[phase, 0],
                send_sem=halo_send,
                recv_sem=halo_recv.at[phase],
                device_id=(s + 1, w),
                device_id_type=MESH,
            )

        def down_copy(phase):
            return pltpu.make_async_remote_copy(
                src_ref=stage.at[phase, 1],
                dst_ref=land.at[phase, 1],
                send_sem=halo_send,
                recv_sem=halo_recv.at[phase],
                device_id=(s - 1, w),
                device_id_type=MESH,
            )

        def send_halo(phase):
            @pl.when(has_down)
            def _():
                down_copy(phase).start()

            @pl.when(has_up)
            def _():
                up_copy(phase).start()

        def settle(sem, many, few):
            @pl.when(inner)
            def _():
                pltpu.make_async_copy(many, many, sem).wait()

            @pl.when(jnp.logical_not(inner))
            def _():
                pltpu.make_async_copy(few, few, sem).wait()

        def take_halo(phase, vf):
            settle(halo_recv.at[phase], land.at[phase], land.at[phase, 0])

            @pl.when(has_down)
            def _():
                for h in range(halo):
                    vf[rows + h] = land[phase, 0, h].astype(F32)

            @pl.when(has_up)
            def _():
                for h in range(halo):
                    vf[rows + halo + h] = land[phase, 1, h].astype(F32)

        def link(off, q):
            named = [got_meta[q, c] for c in range(CAP)]
            at = first_slot + off * CAP
            for c in range(CAP):
                last = latest[named[c]]
                for e in range(c):
                    last = jnp.where(named[e] == named[c], at + e, last)
                before[off * CAP + c] = last
                own_row[off * CAP + c] = jnp.minimum(named[c], rows - 1)
                nbr_row[off * CAP + c] = got_meta[q, CAP + c]
            for r in range(rows):
                last = latest[r]
                for c in range(CAP):
                    last = jnp.where(named[c] == r, at + c, last)
                latest[r] = last

        def unpack(off, q):
            for c in range(CAP):
                own = got[q, c, 0].astype(F32)
                nbr = got[q, c, 1].astype(F32)
                uf[off, c, 0] = own
                uf[off, c, 1] = nbr
                square = jnp.sum(own * own + nbr * nbr, axis=0, keepdims=True)
                speed[off, pl.ds(c, 1), :] = 0.5 + 0.5 * jnp.sqrt(square * (0.5 / width))

        def contract(low, high, vf):
            def some(i, carry):
                at = low + 4 * i
                vectors = jnp.concatenate([vf[at + n].astype(BF16) for n in range(4)], axis=1)
                filled = jnp.dot(form[...], vectors, preferred_element_type=F32)
                flat = jnp.dot(flin[...], jnp.concatenate([vectors, vectors], axis=0), preferred_element_type=F32)
                for n in range(4):
                    bilinear[at + n] = filled[:, n * tile : (n + 1) * tile]
                    linear[at + n] = flat[:, n * tile : (n + 1) * tile]
                return carry

            lax.fori_loop(0, (high - low) // 4, some, 0)

        def applied(off, c, side, row):
            total = linear[row]
            for k in range(width):
                block = bilinear[row, k * width : (k + 1) * width, :]
                total = total + block * jnp.broadcast_to(uf[off, c, side, pl.ds(k, 1), :], (width, tile))
            return total

        def assemble(off, q):
            states = jnp.concatenate([got[q, c, 1] for c in range(CAP)], axis=1)
            ones = jnp.ones((2 * width, CAP * tile), BF16)
            grown = jnp.dot(flux[...], jnp.concatenate([states, ones], axis=0), preferred_element_type=F32)
            for c in range(CAP):
                mats[off, c] = grown[:, c * tile : (c + 1) * tile]

        def neighboured(off, c, vf):
            row = nbr_row[off * CAP + c]
            total = -speed[off, pl.ds(c, 1), :] * vf[row]
            for j in range(width):
                block = mats[off, c, j * width : (j + 1) * width, :]
                total = total + block * jnp.broadcast_to(vf[row, pl.ds(j, 1), :], (width, tile))
            return total

        def first_block(off, q):
            link(off, q)
            unpack(off, q)
            for c in range(CAP):
                row = jnp.minimum(got_meta[q, c], rows - 1)
                nbr = got_meta[q, CAP + c]
                jump = speed[off, pl.ds(c, 1), :] * (vf1[row] - vf1[nbr])
                chain(off, c, (applied(off, c, 0, row) + jump) + applied(off, c, 1, nbr))

        def source(off):
            near = jnp.minimum(w, owners - 1 - w)
            apart = jnp.where(off <= 2 * near, (off + 1) // 2, off - near)
            below = jnp.where(off <= 2 * near, lax.rem(off, 2) == 1, 2 * w >= owners)
            return jnp.where(below, w - apart, w + apart)

        def chain(off, c, term):
            acc[first_slot + off * CAP + c] = term + acc[before[off * CAP + c]]

        def run():
            loads = [
                pltpu.make_async_copy(a, b, in_sem.at[i])
                for i, (a, b) in enumerate(
                    (
                        (dest_hbm, dest_ref),
                        (row_hbm, row_ref),
                        (nbr_hbm, nbr_ref),
                        (fo_hbm, fo),
                        (fn_hbm, fn),
                        (halo_hbm, halo_ref),
                        (res_hbm, res),
                        (quad_hbm, quad),
                        (lin_hbm, lin),
                        (state_hbm, state),
                        (tau_hbm, tau),
                        (rate_hbm, rate),
                        (weight_hbm, weight_ref),
                    )
                )
            ]
            for load in loads[:5]:
                load.start()
            each(1, owners, greet)

            @pl.when(jnp.logical_not(even))
            def _():
                signal(barrier, s - 1, w)

                @pl.when(has_up)
                def _():
                    signal(barrier, s + 1, w)

            for load in loads[5:]:
                load.start()
            around = jnp.where(has_down, 1, 0) + jnp.where(has_up, 1, 0)
            greeted = w + jnp.where(even, around, 0)

            @pl.when(greeted > 0)
            def _():
                pl.semaphore_wait(barrier, greeted)

            each(1, owners, answer)

            @pl.when(even)
            def _():
                @pl.when(has_down)
                def _():
                    signal(halo_ready, s - 1, w)

                @pl.when(has_up)
                def _():
                    signal(halo_ready, s + 1, w)

            for load in loads[:3]:
                load.wait()
            each(0, owners - 1, name_lower)
            for load in loads[3:5]:
                load.wait()
            each(0, owners - 1, send_lower)

            loads[5].wait()
            loads[6].wait()

            def round_rows(r, carry):
                vf1[r] = res[r].astype(BF16).astype(F32)
                return carry

            lax.fori_loop(0, rows, round_rows, 0, unroll=4)
            for h in range(halo):
                stage[0, 0, h] = vf1[halo_ref[0, 0, h]].astype(BF16)
                stage[0, 1, h] = vf1[halo_ref[0, 1, h]].astype(BF16)

            @pl.when(even)
            def _():
                send_halo(0)

            each(1, owners, fill_higher)
            fill_meta(w, got_meta)
            fill_faces(w, got)
            send_higher(1)

            for r in range(rows + 1):
                latest[r] = r
            acc[rows] = jnp.zeros((width, tile), F32)
            for vf in (vf1, vf2):

                @pl.when(s == 0)
                def _():
                    vf[pl.ds(rows, halo)] = jnp.zeros((halo, width, tile), F32)

                @pl.when(s == slabs - 1)
                def _():
                    vf[pl.ds(rows + halo, halo)] = jnp.zeros((halo, width, tile), F32)

            loads[7].wait()
            loads[8].wait()
            at = lax.broadcasted_iota(jnp.int32, (wide, wide), 0)
            column = lax.broadcasted_iota(jnp.int32, (wide, wide), 1)
            swap = jnp.where(column == lax.rem(at, width) * width + at // width, 1.0, 0.0).astype(BF16)
            flux[:, :width] = (
                lax.dot_general(swap, quad[...], (((1,), (1,)), ((), ())), preferred_element_type=F32) * 0.5
            ).astype(BF16)
            half_lin = lin[...] * 0.5
            high = half_lin.astype(BF16)
            low = (half_lin - high.astype(F32)).astype(BF16)
            at = lax.broadcasted_iota(jnp.int32, (wide, width), 0)
            column = lax.broadcasted_iota(jnp.int32, (wide, width), 1)
            pick = jnp.where(column == lax.rem(at, width), 1.0, 0.0).astype(BF16)
            keep = column == at // width
            flin[:, :width] = high
            flin[:, width:] = low
            for i, term in enumerate((high, low)):
                flux[:, (1 + i) * width : (2 + i) * width] = jnp.where(
                    keep, jnp.dot(pick, term, preferred_element_type=F32), 0.0
                ).astype(BF16)
            repeat = jnp.where(column == at // width, 1.0, 0.0).astype(BF16)
            each_state = jnp.dot(repeat, quad[...], preferred_element_type=F32) * 0.5
            at = lax.broadcasted_iota(jnp.int32, (wide, wide), 0)
            column = lax.broadcasted_iota(jnp.int32, (wide, wide), 1)
            each_state = jnp.where(column // width == lax.rem(at, width), each_state, 0.0).astype(BF16)
            at = lax.broadcasted_iota(jnp.int32, (wide, width), 0)
            column = lax.broadcasted_iota(jnp.int32, (wide, width), 1)
            gather = jnp.where(column == lax.rem(at, width), 1.0, 0.0).astype(BF16)
            form[...] = jnp.dot(each_state, gather, preferred_element_type=F32).astype(BF16)

            @pl.when(jnp.logical_not(even))
            def _():
                pl.semaphore_wait(halo_ready, around)
                send_halo(0)

            for load in loads[9:]:
                load.wait()

        run()

        sub = lax.broadcasted_iota(jnp.int32, (width, tile), 0)
        relax = jnp.where(sub == 14, 1.0, 0.0) - jnp.where(sub == 15, 1.0, 0.0)
        mixture = jnp.zeros((width, tile), F32)
        for m in range(nspec):
            mixture = jnp.where(sub == m, weight_ref[m], mixture)

        def prepare(r, carry):
            u = state[r].astype(F32)
            inv = 1.0 / tau[pl.ds(r, 1), :]
            rho = jnp.sum(mixture * u, axis=0, keepdims=True) * inv
            gap = jnp.sum(relax * u, axis=0, keepdims=True) * inv
            coef[r] = gap * mixture + rho * relax
            return carry

        lax.fori_loop(0, rows, prepare, 0, unroll=4)

        def diagonal(vf):
            def one(r, carry):
                v = vf[r]
                change = jnp.sum(coef[r] * v, axis=0, keepdims=True)
                acc[r] = rate[pl.ds(r, 1), :] * v + relax * change
                return carry

            lax.fori_loop(0, rows, one, 0, unroll=4)

        diagonal(vf1)
        each(2, owners, send_higher)

        contract(0, rows, vf1)
        take_halo(0, vf1)
        contract(rows, rows + 2 * halo, vf1)
        first_block(0, w)

        def first_part(off, carry):
            q = source(off)
            pltpu.make_async_copy(got_meta.at[q], got_meta.at[q], meta_recv.at[order(q)]).wait()
            pltpu.make_async_copy(got.at[q], got.at[q], face_recv.at[order(q)]).wait()
            first_block(off, q)
            return carry

        lax.fori_loop(1, owners, first_part, 0)

        for h in range(halo):
            stage[1, 1, h] = acc[latest[halo_ref[0, 1, h]]].astype(BF16)
            stage[1, 0, h] = acc[latest[halo_ref[0, 0, h]]].astype(BF16)
        send_halo(1)
        for r in range(rows):
            value = acc[latest[r]]
            outv1[r] = value
            vf2[r] = value.astype(BF16).astype(F32)
        diagonal(vf2)
        contract(0, rows, vf2)

        def second_own(off, carry):
            for c in range(CAP):
                row = own_row[off * CAP + c]
                part[off * CAP + c] = applied(off, c, 0, row) + speed[off, pl.ds(c, 1), :] * vf2[row]
            assemble(off, source(off))
            return carry

        lax.fori_loop(0, owners, second_own, 0)
        pltpu.make_async_copy(faces.at[pl.ds(0, owners - 1)], faces.at[pl.ds(0, owners - 1)], face_send).wait()
        pltpu.make_async_copy(meta.at[pl.ds(0, owners - 1)], meta.at[pl.ds(0, owners - 1)], meta_send).wait()
        take_halo(1, vf2)

        def second_nbr(off, carry):
            for c in range(CAP):
                chain(off, c, part[off * CAP + c] + neighboured(off, c, vf2))
            return carry

        lax.fori_loop(0, owners, second_nbr, 0, unroll=4)
        for r in range(rows):
            outv2[r] = acc[latest[r]]
        settle(halo_send, stage, stage.at[0])

    dma = pltpu.SemaphoreType.DMA
    pl.run_scoped(scope, dma((13,)), dma(()), dma(()), dma(()))


def store(a, b, c, d, sem):
    first = pltpu.make_async_copy(a, c, sem.at[0])
    second = pltpu.make_async_copy(b, d, sem.at[1])
    first.start()
    second.start()
    first.wait()
    second.wait()


def solution(mesh):
    owners = mesh.shape["wide"]
    slabs = mesh.shape["slab"]

    def on_device(fo, fn, lin, quad, weight, state, tau, rate, res, dest, row, nbr, halo_list):
        count, width, tile = fo.shape
        rows = res.shape[0]
        halo = halo_list.shape[2]
        hbm = pl.BlockSpec(memory_space=pltpu.MemorySpace.HBM)
        vmem = pl.BlockSpec(memory_space=pltpu.MemorySpace.VMEM)
        dma = pltpu.SemaphoreType.DMA
        row_set = (rows, width, tile)
        products = pl.pallas_call(
            functools.partial(kernel, owners, slabs),
            out_shape=(pltpu.VMEM(row_set, F32), pltpu.VMEM(row_set, F32)),
            in_specs=[hbm] * 13,
            out_specs=(vmem, vmem),
            scratch_shapes=[
                pltpu.VMEM(fo.shape, BF16),
                pltpu.VMEM(fn.shape, BF16),
                pltpu.VMEM(lin.shape, F32),
                pltpu.VMEM(quad.shape, BF16),
                pltpu.VMEM(state.shape, BF16),
                pltpu.VMEM(tau.shape, F32),
                pltpu.VMEM(rate.shape, F32),
                pltpu.VMEM(row_set, F32),
                pltpu.VMEM((owners, CAP, 2, width, tile), BF16),
                pltpu.VMEM((owners, CAP, 2, width, tile), BF16),
                pltpu.VMEM((owners, 8, tile), F32),
                pltpu.SMEM((owners, 2 * CAP), jnp.int32),
                pltpu.SMEM((owners, 2 * CAP), jnp.int32),
                pltpu.VMEM((owners, CAP, 2, width, tile), F32),
                pltpu.VMEM((width * width, 3 * width), BF16),
                pltpu.VMEM((width * width, width), BF16),
                pltpu.VMEM((rows + 2 * halo, width * width, tile), F32),
                pltpu.VMEM((rows + 2 * halo, width, tile), F32),
                pltpu.VMEM((width, 2 * width), BF16),
                pltpu.VMEM((owners, CAP, width * width, tile), F32),
                pltpu.VMEM(row_set, F32),
                pltpu.VMEM((rows + 1 + owners * CAP, width, tile), F32),
                pltpu.VMEM((owners * CAP, width, tile), F32),
                pltpu.VMEM((rows + 2 * halo, width, tile), F32),
                pltpu.VMEM((rows + 2 * halo, width, tile), F32),
                pltpu.VMEM((2, 2, halo, width, tile), BF16),
                pltpu.VMEM((2, 2, halo, width, tile), BF16),
                dma((owners - 1,)),
                dma((owners - 1,)),
                dma((2,)),
                pltpu.SemaphoreType.REGULAR((owners - 1,)),
                pltpu.SemaphoreType.REGULAR,
                pltpu.SMEM(weight.shape, F32),
                pltpu.SMEM((count,), jnp.int32),
                pltpu.SMEM(row.shape, jnp.int32),
                pltpu.SMEM(nbr.shape, jnp.int32),
                pltpu.SMEM(halo_list.shape, jnp.int32),
                pltpu.SMEM((rows + 1,), jnp.int32),
                pltpu.SMEM((owners * CAP,), jnp.int32),
                pltpu.SMEM((owners * CAP,), jnp.int32),
                pltpu.SMEM((owners * CAP,), jnp.int32),
                pltpu.SMEM((owners, CAP), jnp.int32),
            ],
            compiler_params=pltpu.CompilerParams(collective_id=0, has_side_effects=True),
        )(fo, fn, lin, quad, weight, state, tau, rate, res, dest.reshape(count), row, nbr, halo_list)
        return pl.pallas_call(
            store,
            out_shape=(jax.ShapeDtypeStruct(row_set, F32), jax.ShapeDtypeStruct(row_set, F32)),
            in_specs=[vmem, vmem],
            out_specs=(hbm, hbm),
            scratch_shapes=[dma((2,))],
        )(*[pltpu.with_memory_space_constraint(x, pltpu.MemorySpace.VMEM) for x in products])

    every = ("slab", "wide")
    cube, flat = P(every, None, None), P(every, None)
    return jax.shard_map(
        on_device,
        mesh=mesh,
        in_specs=(cube, cube, P(), P(), P(), cube, flat, flat, cube, flat, P(every), P(every), cube),
        out_specs=(cube, cube),
        check_vma=False,
    )
```

time: 12.7 us -> 12.5 us (0.984)
  Pallas kernels: 11.9 us -> 11.7 us
    pallas_call x1, Pallas kernels: 11.2 us -> 11 us  [on_device(): pl.pallas_call(functools.partial(kernel, owners, slabs), out_shape=(pltpu...]
where the time goes in v4:
time: 12.5 us; the launch traced here: 12.4 us
  Pallas kernels  11.7 us (94%)
  between operations  0.64 us (5%)
    pallas_call x1, Pallas kernels, on_device(): pl.pallas_call(functools.partial(kernel, owners, slabs), out_shape=(pltpu...  11 us
    pallas_call x1, Pallas kernels, on_device(): pl.pallas_call(store, out_shape=(jax.ShapeDtypeStruct(row_set, F32), jax....  0.72 us

profile of v4, /device:TPU:1, one launch (start us, length us, event | category | flops | bytes accessed | tf_op | source)
XLA Modules:
  0.0 12.4 jit_solution(5542591742748171553)
XLA Ops:
  0.6 11.0 %shard_map.140 = (f32[16,16,128]{2,1,0:T(8,128)S(1)}, f32[16,16,128]{2,1,0:T(8,128)S(1)}) custom-call(bf16[8,16,128]{2,1,0:T(8,128)(2,1)} %fo_hbm.1, bf16[8,16,128]{2,1,0:T(8,128)(2,1)} %fn_hbm.1, f32[16,16]{1,0:T(8,128)} %lin_hbm.1, bf16[16,256]{1,0:T(8,128)(2,1)} %quad_hbm.1, f32[11]{0:T(128)} %weight_hbm.1, bf16[16,16,128]{2,1,0:T(8,128)(2,1)} %state_hbm.1, ...), custom_call_target="tpu_custom_call" | custom-call | tf_op jit(solution)/shard_map/pallas_call | solution.py:557
  11.7 0.7 %shard_map.141 = (f32[16,16,128]{2,1,0:T(8,128)}, f32[16,16,128]{2,1,0:T(8,128)}) custom-call(f32[16,16,128]{2,1,0:T(8,128)S(1)} %get-tuple-element.4.a, f32[16,16,128]{2,1,0:T(8,128)S(1)} %get-tuple-element.5.b), custom_call_target="tpu_custom_call" | custom-call | tf_op jit(solution)/shard_map/pallas_call | solution.py:608

commit v5 on v4

--- a/solution.py
+++ b/solution.py
@@ -278,12 +278,18 @@
 
             lax.fori_loop(0, (high - low) // 4, some, 0)
 
+        def folded(term, low, high):
+            sums = [term(low + n) for n in range(4)]
+            for n in range(low + 4, high):
+                sums[n % 4] = sums[n % 4] + term(n)
+            return (sums[0] + sums[1]) + (sums[2] + sums[3])
+
         def applied(off, c, side, row):
-            total = linear[row]
-            for k in range(width):
+            def term(k):
                 block = bilinear[row, k * width : (k + 1) * width, :]
-                total = total + block * jnp.broadcast_to(uf[off, c, side, pl.ds(k, 1), :], (width, tile))
-            return total
+                return block * jnp.broadcast_to(uf[off, c, side, pl.ds(k, 1), :], (width, tile))
+
+            return linear[row] + folded(term, 0, width)
 
         def assemble(off, q):
             states = jnp.concatenate([got[q, c, 1] for c in range(CAP)], axis=1)
@@ -294,14 +300,14 @@
 
         def neighboured(off, c, vf):
             row = nbr_row[off * CAP + c]
-            total = -speed[off, pl.ds(c, 1), :] * vf[row]
-            for j in range(width):
+
+            def term(j):
                 block = mats[off, c, j * width : (j + 1) * width, :]
-                total = total + block * jnp.broadcast_to(vf[row, pl.ds(j, 1), :], (width, tile))
-            return total
+                return block * jnp.broadcast_to(vf[row, pl.ds(j, 1), :], (width, tile))
+
+            return folded(term, 0, width) - speed[off, pl.ds(c, 1), :] * vf[row]
 
         def first_block(off, q):
-            link(off, q)
             unpack(off, q)
             for c in range(CAP):
                 row = jnp.minimum(got_meta[q, c], rows - 1)
@@ -374,10 +380,16 @@
 
             for load in loads[:3]:
                 load.wait()
-            each(0, owners - 1, name_lower)
+            name_lower(0)
             for load in loads[3:5]:
                 load.wait()
-            each(0, owners - 1, send_lower)
+            send_lower(0)
+
+            def next_lower(peer):
+                name_lower(peer)
+                send_lower(peer)
+
+            each(1, owners - 1, next_lower)
 
             loads[5].wait()
             loads[6].wait()
@@ -485,11 +497,13 @@
         contract(0, rows, vf1)
         take_halo(0, vf1)
         contract(rows, rows + 2 * halo, vf1)
+        link(0, w)
         first_block(0, w)
 
         def first_part(off, carry):
             q = source(off)
             pltpu.make_async_copy(got_meta.at[q], got_meta.at[q], meta_recv.at[order(q)]).wait()
+            link(off, q)
             pltpu.make_async_copy(got.at[q], got.at[q], face_recv.at[order(q)]).wait()
             first_block(off, q)
             return carry
@@ -498,6 +512,7 @@
 
         for h in range(halo):
             stage[1, 1, h] = acc[latest[halo_ref[0, 1, h]]].astype(BF16)
+        for h in range(halo):
             stage[1, 0, h] = acc[latest[halo_ref[0, 0, h]]].astype(BF16)
         send_halo(1)
         for r in range(rows):
@@ -533,13 +548,15 @@
     pl.run_scoped(scope, dma((13,)), dma(()), dma(()), dma(()))
 
 
-def store(a, b, c, d, sem):
-    first = pltpu.make_async_copy(a, c, sem.at[0])
-    second = pltpu.make_async_copy(b, d, sem.at[1])
-    first.start()
-    second.start()
-    first.wait()
-    second.wait()
+def store(a, b, c, d):
+    def run(sem):
+        copies = [pltpu.make_async_copy(a, c, sem.at[0]), pltpu.make_async_copy(b, d, sem.at[1])]
+        for copy in copies:
+            copy.start()
+        for copy in copies:
+            copy.wait()
+
+    pl.run_scoped(run, pltpu.SemaphoreType.DMA((2,)))
 
 
 def solution(mesh):
@@ -610,7 +627,6 @@
             out_shape=(jax.ShapeDtypeStruct(row_set, F32), jax.ShapeDtypeStruct(row_set, F32)),
             in_specs=[vmem, vmem],
             out_specs=(hbm, hbm),
-            scratch_shapes=[dma((2,))],
         )(*[pltpu.with_memory_space_constraint(x, pltpu.MemorySpace.VMEM) for x in products])
 
     every = ("slab", "wide")

time: 12.5 us -> 12.5 us (level)
  no operation moved by 1% of the time
where the time goes in v5:
time: 12.5 us; the launch traced here: 12.3 us
  Pallas kernels  11.7 us (94%)
  between operations  0.64 us (5%)
    pallas_call x1, Pallas kernels, on_device(): pl.pallas_call(functools.partial(kernel, owners, slabs), out_shape=(pltpu...  11 us
    pallas_call x1, Pallas kernels, on_device(): pl.pallas_call(store, out_shape=(jax.ShapeDtypeStruct(row_set, F32), jax....  0.7 us

profile of v5, /device:TPU:1, one launch (start us, length us, event | category | flops | bytes accessed | tf_op | source)
XLA Modules:
  0.0 12.3 jit_solution(11732934240065627089)
XLA Ops:
  0.6 11.0 %shard_map.140 = (f32[16,16,128]{2,1,0:T(8,128)S(1)}, f32[16,16,128]{2,1,0:T(8,128)S(1)}) custom-call(bf16[8,16,128]{2,1,0:T(8,128)(2,1)} %fo_hbm.1, bf16[8,16,128]{2,1,0:T(8,128)(2,1)} %fn_hbm.1, f32[16,16]{1,0:T(8,128)} %lin_hbm.1, bf16[16,256]{1,0:T(8,128)(2,1)} %quad_hbm.1, f32[11]{0:T(128)} %weight_hbm.1, bf16[16,16,128]{2,1,0:T(8,128)(2,1)} %state_hbm.1, ...), custom_call_target="tpu_custom_call" | custom-call | tf_op jit(solution)/shard_map/pallas_call | solution.py:574
  11.6 0.7 %shard_map.141 = (f32[16,16,128]{2,1,0:T(8,128)}, f32[16,16,128]{2,1,0:T(8,128)}) custom-call(f32[16,16,128]{2,1,0:T(8,128)S(1)} %get-tuple-element.4.a, f32[16,16,128]{2,1,0:T(8,128)S(1)} %get-tuple-element.5.b), custom_call_target="tpu_custom_call" | custom-call | tf_op jit(solution)/shard_map/pallas_call | solution.py:625

commit v6 on v5

--- a/solution.py
+++ b/solution.py
@@ -133,8 +133,8 @@
                 place[d, c] = jnp.where(found[c] > 0, row_ref[source], rows)
                 place[d, CAP + c] = jnp.where(found[c] > 0, nbr_ref[source], 0)
 
-        def fill_faces(d, place):
-            for c in range(CAP):
+        def fill_faces(d, place, low=0, some=CAP):
+            for c in range(low, low + some):
                 source = picked[d, c]
                 place[d, c, 0] = fo[source]
                 place[d, c, 1] = fn[source]
@@ -142,10 +142,10 @@
         def order(peer):
             return peer - jnp.where(peer > w, 1, 0)
 
-        def face_copy(peer):
+        def face_copy(peer, c, some):
             return pltpu.make_async_remote_copy(
-                src_ref=faces.at[peer],
-                dst_ref=got.at[w],
+                src_ref=faces.at[peer, pl.ds(c, some)],
+                dst_ref=got.at[w, pl.ds(c, some)],
                 send_sem=face_send,
                 recv_sem=face_recv.at[w - jnp.where(w > peer, 1, 0)],
                 device_id=(s, peer),
@@ -171,8 +171,9 @@
         def send_lower(peer):
             @pl.when(peer < w)
             def _():
-                fill_faces(peer, faces)
-                face_copy(peer).start()
+                for c in range(0, CAP, 2):
+                    fill_faces(peer, faces, c, 2)
+                    face_copy(peer, c, 2).start()
 
         def fill_higher(off):
             @pl.when(w + off < owners)
@@ -187,22 +188,23 @@
             def _():
                 pl.semaphore_wait(ready.at[peer - 1], 1)
                 meta_copy(peer).start()
-                face_copy(peer).start()
-
-        def up_copy(phase):
+                for c in range(0, CAP, 2):
+                    face_copy(peer, c, 2).start()
+
+        def up_copy(phase, h, some):
             return pltpu.make_async_remote_copy(
-                src_ref=stage.at[phase, 0],
-                dst_ref=land.at[phase, 0],
+                src_ref=stage.at[phase, 0, pl.ds(h, some)],
+                dst_ref=land.at[phase, 0, pl.ds(h, some)],
                 send_sem=halo_send,
                 recv_sem=halo_recv.at[phase],
                 device_id=(s + 1, w),
                 device_id_type=MESH,
             )
 
-        def down_copy(phase):
+        def down_copy(phase, h, some):
             return pltpu.make_async_remote_copy(
-                src_ref=stage.at[phase, 1],
-                dst_ref=land.at[phase, 1],
+                src_ref=stage.at[phase, 1, pl.ds(h, some)],
+                dst_ref=land.at[phase, 1, pl.ds(h, some)],
                 send_sem=halo_send,
                 recv_sem=halo_recv.at[phase],
                 device_id=(s - 1, w),
@@ -212,11 +214,13 @@
         def send_halo(phase):
             @pl.when(has_down)
             def _():
-                down_copy(phase).start()
+                for h in range(0, halo, 2):
+                    down_copy(phase, h, min(2, halo - h)).start()
 
             @pl.when(has_up)
             def _():
-                up_copy(phase).start()
+                for h in range(0, halo, 2):
+                    up_copy(phase, h, min(2, halo - h)).start()
 
         def settle(sem, many, few):
             @pl.when(inner)

time: 12.5 us -> 12.5 us (level)
  no operation moved by 1% of the time
where the time goes in v6:
time: 12.5 us; the launch traced here: 12.3 us
  Pallas kernels  11.7 us (94%)
  between operations  0.64 us (5%)
    pallas_call x1, Pallas kernels, on_device(): pl.pallas_call(functools.partial(kernel, owners, slabs), out_shape=(pltpu...  11 us
    pallas_call x1, Pallas kernels, on_device(): pl.pallas_call(store, out_shape=(jax.ShapeDtypeStruct(row_set, F32), jax....  0.7 us

profile of v6, /device:TPU:1, one launch (start us, length us, event | category | flops | bytes accessed | tf_op | source)
XLA Modules:
  0.0 12.3 jit_solution(9002654919134714849)
XLA Ops:
  0.6 11.0 %shard_map.140 = (f32[16,16,128]{2,1,0:T(8,128)S(1)}, f32[16,16,128]{2,1,0:T(8,128)S(1)}) custom-call(bf16[8,16,128]{2,1,0:T(8,128)(2,1)} %fo_hbm.1, bf16[8,16,128]{2,1,0:T(8,128)(2,1)} %fn_hbm.1, f32[16,16]{1,0:T(8,128)} %lin_hbm.1, bf16[16,256]{1,0:T(8,128)(2,1)} %quad_hbm.1, f32[11]{0:T(128)} %weight_hbm.1, bf16[16,16,128]{2,1,0:T(8,128)(2,1)} %state_hbm.1, ...), custom_call_target="tpu_custom_call" | custom-call | tf_op jit(solution)/shard_map/pallas_call | solution.py:578
  11.6 0.7 %shard_map.141 = (f32[16,16,128]{2,1,0:T(8,128)}, f32[16,16,128]{2,1,0:T(8,128)}) custom-call(f32[16,16,128]{2,1,0:T(8,128)S(1)} %get-tuple-element.4.a, f32[16,16,128]{2,1,0:T(8,128)S(1)} %get-tuple-element.5.b), custom_call_target="tpu_custom_call" | custom-call | tf_op jit(solution)/shard_map/pallas_call | solution.py:629
